TPU v7x, 32 devices: a whole 2x2x4 slice. The times are simulated.
32 devices in a mesh: lat: 8 (over z, y), lon: 4 (over x, core).
Axes of the slice: x: 2, y: 2, z: 4, core: 2. Of those that a mesh axis runs over, the one named last changes fastest.
Arguments:
- fields: bfloat16 [69, 128, 512], P(None, 'lat', 'lon'), may hold values from -6 to 6
- enc_kernel: bfloat16 [3, 3, 256, 69], replicated, may hold values from -0.25 to 0.25
- gen_kernel: bfloat16 [3, 3, 69, 256], replicated, may hold values from -0.125 to 0.125
- recon_grad: bfloat16 [69, 128, 512], P(None, 'lat', 'lon'), may hold values from -6 to 6
Outputs:
- rebuilt: bfloat16 [69, 128, 512], P(None, 'lat', 'lon')
- feat_grad: bfloat16 [256, 128, 512], P(None, 'lat', 'lon')
- enc_grad: float32 [3, 3, 256, 69], replicated
- gen_grad: float32 [3, 3, 69, 256], replicated
All inputs are finite; a program needn't handle non-finite values.
Results may differ from a plain program's by a relative error of at most 0.0085.
Values may be sent and summed in bfloat16 or wider, within the bound.
A program may use at most 64 MiB of HBM per device.

v0:
```python
import jax
import jax.numpy as jnp
from jax import lax
from jax.sharding import PartitionSpec as P


def extended(cells, sides, width, closed):
    for axis, dim in sides:
        count = lax.axis_size(axis)
        ends = count if closed else count - 1
        head = lax.slice_in_dim(cells, 0, width, axis=dim)
        tail = lax.slice_in_dim(cells, cells.shape[dim] - width, cells.shape[dim], axis=dim)
        cells = jnp.concatenate(
            [
                lax.ppermute(tail, axis, [(i, (i + 1) % count) for i in range(ends)]),
                cells,
                lax.ppermute(head, axis, [((i + 1) % count, i) for i in range(ends)]),
            ],
            axis=dim,
        )
    return cells


def from_behind(value, axis, steps):
    count = lax.axis_size(axis)
    pairs = [(source, (source + steps) % count) for source in range(count)]
    return lax.ppermute(value, axis, pairs)


def face_pad(source):
    lon_count = lax.axis_size("lon")
    widened = extended(source, (("lon", 2),), 1, True)
    edge_rows = jnp.concatenate([widened[:, :1], widened[:, -1:]], axis=1)
    pole_rows = from_behind(edge_rows, "lon", lon_count // 2)
    plain_pad = extended(widened, (("lat", 1),), 1, False)
    result = (plain_pad, pole_rows)
    return result


def with_poles(plain_pad, pole_rows):
    lat_index = lax.axis_index("lat")
    lat_count = lax.axis_size("lat")
    upper = jnp.where(lat_index == 0, pole_rows[:, :1], plain_pad[:, :1])
    lower = jnp.where(lat_index == lat_count - 1, pole_rows[:, 1:], plain_pad[:, -1:])
    return jnp.concatenate([upper, plain_pad[:, 1:-1], lower], axis=1)


def convolve(padded, kernel, height, width):
    running = None
    for row_tap in range(3):
        for col_tap in range(3):
            section = padded[:, row_tap : row_tap + height, col_tap : col_tap + width].reshape(
                padded.shape[0], height * width
            )
            product = jnp.dot(kernel[row_tap, col_tap], section, preferred_element_type=jnp.float32)
            running = product if running is None else running + product
    return running.reshape(kernel.shape[2], height, width)


def adjoint_conv(padded, kernel, height, width):
    running = None
    for row_tap in range(3):
        for col_tap in range(3):
            section = padded[
                :, 2 - row_tap : 2 - row_tap + height, 2 - col_tap : 2 - col_tap + width
            ].reshape(padded.shape[0], height * width)
            product = lax.dot_general(
                kernel[row_tap, col_tap],
                section,
                (((0,), (0,)), ((), ())),
                preferred_element_type=jnp.float32,
            )
            running = product if running is None else running + product
    return running.reshape(kernel.shape[3], height, width)


def pole_terms(pole_rows, kernel, width):
    terms = []
    for which, row_tap in ((0, 0), (1, 2)):
        running = None
        for col_tap in range(3):
            section = pole_rows[:, which, 2 - col_tap : 2 - col_tap + width]
            product = lax.dot_general(
                kernel[row_tap, col_tap],
                section,
                (((0,), (0,)), ((), ())),
                preferred_element_type=jnp.float32,
            )
            running = product if running is None else running + product
        terms.append(running)
    return (terms[0], terms[1])


def weight_grad(cotangent, padded, height, width):
    flat_cot = cotangent.reshape(cotangent.shape[0], height * width)
    taps = []
    for row_tap in range(3):
        row_list = []
        for col_tap in range(3):
            section = padded[:, row_tap : row_tap + height, col_tap : col_tap + width].reshape(
                padded.shape[0], height * width
            )
            row_list.append(
                lax.dot_general(
                    flat_cot, section, (((1,), (1,)), ((), ())), preferred_element_type=jnp.float32
                )
            )
        taps.append(jnp.stack(row_list))
    return jnp.stack(taps)


def sum_grads(enc_part, gen_part):
    summed = lax.psum((enc_part, gen_part), ("lat", "lon"))
    return summed


def on_device(fields, enc_kernel, gen_kernel, recon_grad):
    height = fields.shape[1]
    width = fields.shape[2]
    in_count = fields.shape[0]
    lat_index = lax.axis_index("lat")
    lat_count = lax.axis_size("lat")
    lon_count = lax.axis_size("lon")
    plain_pair, pole_pair = face_pad(jnp.concatenate([fields, recon_grad], axis=0))
    plain_in = plain_pair[:in_count]
    pole_in = pole_pair[:in_count]
    plain_cot = plain_pair[in_count:]
    pole_cot = pole_pair[in_count:]
    padded_in = with_poles(plain_in, pole_in)
    pre_act = convolve(padded_in, enc_kernel, height, width)
    hidden = jax.nn.silu(pre_act).astype(jnp.bfloat16)
    plain_hid, pole_hid = face_pad(hidden)
    padded_hid = with_poles(plain_hid, pole_hid)
    rebuilt = convolve(padded_hid, gen_kernel, height, width).astype(jnp.bfloat16)
    feat_f32 = adjoint_conv(plain_cot, gen_kernel, height, width)
    upper_term, lower_term = pole_terms(pole_cot, gen_kernel, width)
    feat_f32 = feat_f32.at[:, 0].add(jnp.where(lat_index == 0, upper_term, 0.0))
    feat_f32 = feat_f32.at[:, -1].add(jnp.where(lat_index == lat_count - 1, lower_term, 0.0))
    feat_grad = feat_f32.astype(jnp.bfloat16)
    logistic = jax.nn.sigmoid(pre_act)
    pre_grad = (
        feat_grad.astype(jnp.float32) * logistic * (1.0 + pre_act * (1.0 - logistic))
    ).astype(jnp.bfloat16)
    gen_part = weight_grad(recon_grad, padded_hid, height, width)
    enc_part = weight_grad(pre_grad, padded_in, height, width)
    enc_sum, gen_sum = sum_grads(enc_part, gen_part)
    norm_scale = 1.0 / jnp.sqrt(jnp.float32(height * lat_count * width * lon_count))
    return (rebuilt, feat_grad, enc_sum * norm_scale, gen_sum * norm_scale)


def solution(mesh):
    return jax.shard_map(
        on_device,
        mesh=mesh,
        in_specs=(P(None, "lat", "lon"), P(), P(), P(None, "lat", "lon")),
        out_specs=(P(None, "lat", "lon"), P(None, "lat", "lon"), P(), P()),
        check_vma=False,
    )
```

profile of v0, /device:TPU:0, one launch (start us, length us, event | category | flops | bytes accessed | tf_op | source)
XLA Modules:
  0.0 219.3 jit_solution(15706340045346851141)
XLA Ops:
  7.2 1.1 copy.90
  8.3 1.1 copy.91
  10.1 2.4 %collective-permute-start.1 = (bf16[138,16,1]{0,1,2:T(8,128)(2,1)S(1)}, bf16[138,16,1]{0,1,2:T(8,128)(2,1)S(1)}, u32[]{:S(2)}, u32[]{:S(2)}) collective-permute-start(bf16[138,16,1]{0,1,2:T(8,128)(2,1)S(1)} %copy.93), channel_id=1, source_target_pairs={{1,0},{2,1},{3,2},{0,3},{5,4},{6,5},{7,6},{4,7},{9,8},{10,9},{11,1... | collective-permute-start | bytes 13256 | tf_op jit(solution)/shard_map/ppermute | solution.py:17
  13.3 0.7 collective-permute-done.1
  14.3 1.8 collective-permute-done
  16.9 0.5 pad_maximum_fusion.17
  17.5 1.3 collective-permute-start.4
  18.8 4.7 %collective-permute-start.3 = (bf16[138,1,130]{2,0,1:T(8,128)(2,1)S(1)}, bf16[138,1,130]{2,0,1:T(8,128)(2,1)S(1)}, u32[]{:S(2)}, u32[]{:S(2)}) collective-permute-start(bf16[138,1,130]{2,0,1:T(8,128)(2,1)S(1)} %get-tuple-element.52), channel_id=1, source_target_pairs={{0,4},{4,8},{8,12},{12,16},{16,20},{20,24},{24,28},{1,5},{5,9},{9,... | collective-permute-start | bytes 107648 | tf_op jit(solution)/shard_map/ppermute | solution.py:15
  23.5 0.6 collective-permute-start.2
  24.5 0.8 pad_maximum_fusion.19
  25.4 0.9 pad_maximum_fusion.9
  27.4 0.6 copy-done.6
  27.9 0.5 fusion.55
  30.9 0.5 fusion.2
  31.4 0.5 fusion.1
  31.9 0.5 fusion
  34.0 0.6 copy-done.8
  36.5 0.5 convolution_add_fusion.4
  37.0 0.5 fusion.8
  37.5 0.5 fusion.7
  38.0 0.5 fusion.6
  38.5 0.7 fusion.5
  39.2 1.5 fusion.23
  42.3 0.9 multiply_convert_fusion
  45.7 0.6 fusion.121
  47.0 1.7 collective-permute-start.6
  48.8 0.9 pad_maximum_fusion.3
  49.7 1.8 copy.144
  51.5 4.4 %collective-permute-start.8 = (bf16[256,1,130]{0,2,1:T(8,128)(2,1)S(1)}, bf16[256,1,130]{0,2,1:T(8,128)(2,1)S(1)}, u32[]{:S(2)}, u32[]{:S(2)}) collective-permute-start(bf16[256,1,130]{0,2,1:T(8,128)(2,1)S(1)} %get-tuple-element.65), channel_id=1, source_target_pairs={{0,4},{4,8},{8,12},{12,16},{16,20},{20,24},{24,28},{1,5},{5,9},{9,... | collective-permute-start | bytes 199688 | tf_op jit(solution)/shard_map/ppermute | solution.py:15
  55.9 1.3 collective-permute-start.9
  57.2 1.5 collective-permute-start.7
  58.7 0.6 pad_maximum_fusion.1
  60.0 3.3 %collective-permute-done.9 = bf16[256,1,130]{0,2,1:T(8,128)(2,1)S(1)} collective-permute-done((bf16[256,1,130]{0,2,1:T(8,128)(2,1)S(1)}, bf16[256,1,130]{0,2,1:T(8,128)(2,1)S(1)}, u32[]{:S(2)}, u32[]{:S(2)}) %collective-permute-start.9) | collective-permute-done | bytes 66592 | tf_op jit(solution)/shard_map/ppermute | solution.py:17
  63.2 0.7 maximum_maximum_fusion
  66.1 3.3 %fusion.119 = (bf16[256,16,128]{0,2,1:T(8,128)(2,1)}, bf16[256,16,128]{0,2,1:T(8,128)(2,1)S(1)}, bf16[256,16,128]{0,2,1:T(8,128)(2,1)S(1)}, bf16[256,16,128]{0,2...) fusion(bf16[256,17,130]{0,2,1:T(8,128)(2,1)S(1)} %get-tuple-element.64, ...), kind=kLoop, calls=%fused_computation.229 | loop fusion | bytes 12582912 | tf_op jit(solution)/shard_map/slice | solution.py:52
  69.4 2.0 fusion.38
  71.4 2.0 fusion.57
  73.5 0.9 pad_maximum_fusion.4
  74.4 2.0 convolution_add_fusion.13
  76.4 1.3 convolution_add_fusion.12
  77.7 1.2 fusion.10
  79.0 1.3 fusion.11
  80.3 1.2 convolution_add_fusion.9
  81.5 1.2 fusion.12
  82.8 0.7 slice.427
  83.5 125.0 %all-reduce.3.cloned.1.call-done = (f32[3,3,256,69]{2,3,1,0:T(8,128)}, f32[3,3,69,256]{3,2,1,0:T(8,128)}) async-done(((f32[3,3,256,69]{2,3,1,0:T(8,128)}, f32[3,3,69,256]{3,2,1,0:T(8,128)}), (f32[3,3,256,69]{2,3,1,0:T(8,128)}, f32[3,3,69,256]{3,2,1,0:T(8,128)})) %all-reduce.3.cloned.1.call-update) | async-done | bytes 1271824 | tf_op jit(solution)/shard_map/psum | solution.py:113
  208.5 2.0 broadcast_multiply_fusion.1
  210.5 2.0 broadcast_multiply_fusion
  (130 shorter events, 17.3 us)
Async XLA Ops:
  7.2 5.8 %copy-start.3 = (bf16[69,16,128]{2,1,0:T(8,128)(2,1)S(1)}, bf16[69,16,128]{2,1,0:T(8,128)(2,1)}, u32[]{:S(2)}) copy-start(bf16[69,16,128]{2,1,0:T(8,128)(2,1)} %param.8) | copy-start | bytes 847876
  7.2 201.4 %all-reduce.3.cloned.1.call-start = ((), (), s32[]{:S(2)}) async-start(), calls=%async_computation | async-start | bytes 2654208 | tf_op jit(solution)/shard_map/psum | solution.py:113
  8.3 4.7 %copy-start = (bf16[69,16,128]{2,1,0:T(8,128)(2,1)S(1)}, bf16[69,16,128]{2,1,0:T(8,128)(2,1)}, u32[]{:S(2)}) copy-start(bf16[69,16,128]{2,1,0:T(8,128)(2,1)} %param.11) | copy-start | bytes 847876
  10.1 3.8 %collective-permute-start.1 = (bf16[138,16,1]{0,1,2:T(8,128)(2,1)S(1)}, bf16[138,16,1]{0,1,2:T(8,128)(2,1)S(1)}, u32[]{:S(2)}, u32[]{:S(2)}) collective-permute-start(bf16[138,16,1]{0,1,2:T(8,128)(2,1)S(1)} %copy.93), channel_id=1, source_target_pairs={{1,0},{2,1},{3,2},{0,3},{5,4},{6,5},{7,6},{4,7},{9,8},{10,9},{11,1... | collective-permute-start | bytes 13256 | tf_op jit(solution)/shard_map/ppermute | solution.py:17
  12.9 3.1 %collective-permute-start = (bf16[138,16,1]{0,1,2:T(8,128)(2,1)S(1)}, bf16[138,16,1]{0,1,2:T(8,128)(2,1)S(1)}, u32[]{:S(2)}, u32[]{:S(2)}) collective-permute-start(bf16[138,16,1]{0,1,2:T(8,128)(2,1)S(1)} %copy.92), channel_id=1, source_target_pairs={{0,1},{1,2},{2,3},{3,0},{4,5},{5,6},{6,7},{7,4},{8,9},{9,10},{10,1... | collective-permute-start | bytes 13256 | tf_op jit(solution)/shard_map/ppermute | solution.py:15
  17.5 7.0 %collective-permute-start.4 = (bf16[138,1,130]{2,0,1:T(8,128)(2,1)S(1)}, bf16[138,1,130]{2,0,1:T(8,128)(2,1)S(1)}, u32[]{:S(2)}, u32[]{:S(2)}) collective-permute-start(bf16[138,1,130]{2,0,1:T(8,128)(2,1)S(1)} %get-tuple-element.51), channel_id=1, source_target_pairs={{4,0},{8,4},{12,8},{16,12},{20,16},{24,20},{28,24},{5,1},{9,5},{13... | collective-permute-start | bytes 107648 | tf_op jit(solution)/shard_map/ppermute | solution.py:17
  18.8 6.6 %collective-permute-start.3 = (bf16[138,1,130]{2,0,1:T(8,128)(2,1)S(1)}, bf16[138,1,130]{2,0,1:T(8,128)(2,1)S(1)}, u32[]{:S(2)}, u32[]{:S(2)}) collective-permute-start(bf16[138,1,130]{2,0,1:T(8,128)(2,1)S(1)} %get-tuple-element.52), channel_id=1, source_target_pairs={{0,4},{4,8},{8,12},{12,16},{16,20},{20,24},{24,28},{1,5},{5,9},{9,... | collective-permute-start | bytes 107648 | tf_op jit(solution)/shard_map/ppermute | solution.py:15
  23.5 9.0 %collective-permute-start.2 = (bf16[138,2,130]{2,0,1:T(8,128)(2,1)S(1)}, bf16[138,2,130]{2,0,1:T(8,128)(2,1)S(1)}, u32[]{:S(2)}, u32[]{:S(2)}) collective-permute-start(bf16[138,2,130]{2,0,1:T(8,128)(2,1)S(1)} %pad_maximum_fusion.29), channel_id=1, source_target_pairs={{0,2},{1,3},{2,0},{3,1},{4,6},{5,7},{6,4},{7,5},{8,10},{9,11},{10,... | collective-permute-start | bytes 215288 | tf_op jit(solution)/shard_map/ppermute | solution.py:27
  27.0 1.0 copy-start.6
  33.6 1.0 copy-start.8
  45.1 1.5 copy-start.4
  46.9 4.5 %collective-permute-start.5 = (bf16[256,16,1]{0,2,1:T(2,128)(2,1)}, bf16[256,16,1]{0,2,1:T(2,128)(2,1)S(1)}, u32[]{:S(2)}, u32[]{:S(2)}) collective-permute-start(bf16[256,16,1]{0,2,1:T(2,128)(2,1)} %get-tuple-element.69), channel_id=1, source_target_pairs={{0,1},{1,2},{2,3},{3,0},{4,5},{5,6},{6,7},{7,4},{8,9},{9,10},{10,1... | collective-permute-start | bytes 24584 | tf_op jit(solution)/shard_map/ppermute | solution.py:15
  47.0 4.5 %collective-permute-start.6 = (bf16[256,16,1]{0,2,1:T(2,128)(2,1)S(1)}, bf16[256,16,1]{0,2,1:T(2,128)(2,1)S(1)}, u32[]{:S(2)}, u32[]{:S(2)}) collective-permute-start(bf16[256,16,1]{0,2,1:T(2,128)(2,1)S(1)} %get-tuple-element.70), channel_id=1, source_target_pairs={{1,0},{2,1},{3,2},{0,3},{5,4},{6,5},{7,6},{4,7},{9,8},{10,9},{11,1... | collective-permute-start | bytes 24584 | tf_op jit(solution)/shard_map/ppermute | solution.py:17
  51.5 8.4 %collective-permute-start.8 = (bf16[256,1,130]{0,2,1:T(8,128)(2,1)S(1)}, bf16[256,1,130]{0,2,1:T(8,128)(2,1)S(1)}, u32[]{:S(2)}, u32[]{:S(2)}) collective-permute-start(bf16[256,1,130]{0,2,1:T(8,128)(2,1)S(1)} %get-tuple-element.65), channel_id=1, source_target_pairs={{0,4},{4,8},{8,12},{12,16},{16,20},{20,24},{24,28},{1,5},{5,9},{9,... | collective-permute-start | bytes 199688 | tf_op jit(solution)/shard_map/ppermute | solution.py:15
  55.9 7.3 %collective-permute-start.9 = (bf16[256,1,130]{0,2,1:T(8,128)(2,1)S(1)}, bf16[256,1,130]{0,2,1:T(8,128)(2,1)S(1)}, u32[]{:S(2)}, u32[]{:S(2)}) collective-permute-start(bf16[256,1,130]{0,2,1:T(8,128)(2,1)S(1)} %get-tuple-element.66), channel_id=1, source_target_pairs={{4,0},{8,4},{12,8},{16,12},{20,16},{24,20},{28,24},{5,1},{9,5},{13... | collective-permute-start | bytes 199688 | tf_op jit(solution)/shard_map/ppermute | solution.py:17
  57.2 6.0 %collective-permute-start.7 = (bf16[256,2,130]{0,2,1:T(8,128)(2,1)S(1)}, bf16[256,2,130]{0,2,1:T(8,128)(2,1)S(1)}, u32[]{:S(2)}, u32[]{:S(2)}) collective-permute-start(bf16[256,2,130]{0,2,1:T(8,128)(2,1)S(1)} %pad_maximum_fusion.30), channel_id=1, source_target_pairs={{0,2},{1,3},{2,0},{3,1},{4,6},{5,7},{6,4},{7,5},{8,10},{9,11},{10,... | collective-permute-start | bytes 399368 | tf_op jit(solution)/shard_map/ppermute | solution.py:27
  74.4 2.0 copy-start.1
  74.4 3.3 %copy-start.7 = (f32[2048,69]{0,1:T(8,128)S(1)}, f32[2048,69]{0,1:T(8,128)}, u32[]{:S(2)}) copy-start(f32[2048,69]{0,1:T(8,128)} %fusion.23) | copy-start | bytes 1695748
  76.4 2.5 %copy-start.5 = (f32[2048,69]{0,1:T(8,128)S(1)}, f32[2048,69]{0,1:T(8,128)}, u32[]{:S(2)}) copy-start(f32[2048,69]{0,1:T(8,128)} %fusion.38) | copy-start | bytes 1695748
  78.9 2.5 %copy-start.2 = (bf16[256,16,128]{0,2,1:T(8,128)(2,1)S(1)}, bf16[256,16,128]{0,2,1:T(8,128)(2,1)}, u32[]{:S(2)}) copy-start(bf16[256,16,128]{0,2,1:T(8,128)(2,1)} %get-tuple-element.53) | copy-start | bytes 3145732
Sparse Core Ops, SparseCore 0:
  74.5 133.9 all-reduce.2
where the time goes:
time: 220 us; the launch traced here: 219 us
  waiting for transfers between devices  131 us (60%)
  matrix products  30 us (14%)
  starting transfers between devices  18.1 us (8%)
  between operations  15 us (7%)
  local copies, waits for them, and re-layouts  13.7 us (6%)
  other arithmetic  11.7 us (5%)
    psum x1, waiting for transfers between devices, sum_grads(): summed = lax.psum((enc_part, gen_part), ('lat', 'lon'))  125 us
    dot_general x18, matrix products, convolve(): jnp.dot(kernel[row_tap, col_tap], section, preferred_element_type=jnp.flo...  18.4 us
    ppermute x4, starting transfers between devices, extended(): lax.ppermute(tail, axis, [(i, (i + 1) % count) for i in range(ends)])  9.17 us
    unnamed x58, local copies, waits for them, and re-layouts  6.96 us
    ppermute x4, starting transfers between devices, extended(): lax.ppermute(head, axis, [((i + 1) % count, i) for i in range(ends)])  6.75 us
    dot_general x18, matrix products, weight_grad(): lax.dot_general(flat_cot, section, (((1,), (1,)), ((), ())), preferred_el...  5.67 us
  transfers between devices with their start and end apart: 11, of which 4 were waited for; matrix products, arithmetic and copies ran while one was open for 10% of the time, Pallas kernels for 0%

commit v1 on v0

v1 whole, which is shorter than its diff:
```python
import functools

import jax
import jax.numpy as jnp
from jax import lax
from jax.experimental import pallas as pl
from jax.experimental.pallas import tpu as pltpu
from jax.sharding import PartitionSpec as P

MESH = pl.DeviceIdType.MESH
SEND = jnp.float32


def extended(cells, sides, width, closed):
    for axis, dim in sides:
        count = lax.axis_size(axis)
        ends = count if closed else count - 1
        head = lax.slice_in_dim(cells, 0, width, axis=dim)
        tail = lax.slice_in_dim(cells, cells.shape[dim] - width, cells.shape[dim], axis=dim)
        cells = jnp.concatenate(
            [
                lax.ppermute(tail, axis, [(i, (i + 1) % count) for i in range(ends)]),
                cells,
                lax.ppermute(head, axis, [((i + 1) % count, i) for i in range(ends)]),
            ],
            axis=dim,
        )
    return cells


def from_behind(value, axis, steps):
    count = lax.axis_size(axis)
    pairs = [(source, (source + steps) % count) for source in range(count)]
    return lax.ppermute(value, axis, pairs)


def face_pad(source):
    lon_count = lax.axis_size("lon")
    widened = extended(source, (("lon", 2),), 1, True)
    edge_rows = jnp.concatenate([widened[:, :1], widened[:, -1:]], axis=1)
    pole_rows = from_behind(edge_rows, "lon", lon_count // 2)
    plain_pad = extended(widened, (("lat", 1),), 1, False)
    return (plain_pad, pole_rows)


def with_poles(plain_pad, pole_rows):
    lat_index = lax.axis_index("lat")
    lat_count = lax.axis_size("lat")
    upper = jnp.where(lat_index == 0, pole_rows[:, :1], plain_pad[:, :1])
    lower = jnp.where(lat_index == lat_count - 1, pole_rows[:, 1:], plain_pad[:, -1:])
    return jnp.concatenate([upper, plain_pad[:, 1:-1], lower], axis=1)


def reduce_kernel(lats, halves, a_ref, out_ref, from_pair, held_pair, from_lon, held_lon, from_lat, *sems):
    lat = lax.axis_index("lat")
    lon = lax.axis_index("lon")
    half = lax.div(lon, 2)
    core = lax.rem(lon, 2)
    other = 1 - core

    def lon_peer(step):
        return (lat, lax.rem(half + step, halves) * 2 + core)

    def lat_peer(step):
        return (lax.rem(lat + step, lats), lon)

    pair = (lat, half * 2 + other)
    barrier = pltpu.get_barrier_semaphore()
    peers = [pair]
    peers += [lon_peer(step) for step in range(1, halves)]
    peers += [lat_peer(step) for step in range(1, lats)]
    for peer in peers:
        pl.semaphore_signal(barrier, inc=1, device_id=peer, device_id_type=MESH)
    pl.semaphore_wait(barrier, len(peers))

    def send(src, dst, phase, slot, peer):
        copy = pltpu.make_async_remote_copy(
            src_ref=src,
            dst_ref=dst,
            send_sem=sems[2 * phase].at[slot],
            recv_sem=sems[2 * phase + 1].at[slot],
            device_id=peer,
            device_id_type=MESH,
        )
        copy.start()
        return copy

    send(a_ref.at[other], from_pair, 0, 0, pair).wait()
    held_pair[...] = (a_ref[core].astype(jnp.float32) + from_pair[...].astype(jnp.float32)).astype(
        held_pair.dtype
    )
    copies = []
    for step in range(1, halves):
        target = lax.rem(half + step, halves)
        copies.append(send(held_pair.at[target], from_lon.at[step - 1], 1, step - 1, lon_peer(step)))
    for copy in copies:
        copy.wait()
    total = held_pair[half].astype(jnp.float32)
    for step in range(1, halves):
        total = total + from_lon[step - 1].astype(jnp.float32)
    held_lon[...] = total.astype(held_lon.dtype)
    copies = []
    for step in range(1, lats):
        target = lax.rem(lat + step, lats)
        copies.append(send(held_lon.at[target], from_lat.at[step - 1], 2, step - 1, lat_peer(step)))
    for copy in copies:
        copy.wait()
    total = held_lon[lat].astype(jnp.float32)
    for step in range(1, lats):
        total = total + from_lat[step - 1].astype(jnp.float32)
    out_ref[core, half, lat] = total.astype(out_ref.dtype)
    mine = out_ref.at[core, half, lat]
    copies = [send(mine, mine, 3, step - 1, lat_peer(step)) for step in range(1, lats)]
    for copy in copies:
        copy.wait()
    mine = out_ref.at[core, half]
    copies = [send(mine, mine, 4, step - 1, lon_peer(step)) for step in range(1, halves)]
    for copy in copies:
        copy.wait()
    mine = out_ref.at[core]
    send(mine, mine, 5, 0, pair).wait()


def reduce_all(stacked):
    lats = lax.axis_size("lat")
    halves = lax.axis_size("lon") // 2
    rows, width = stacked.shape
    unit = 16
    piece = -(-rows // (2 * halves * lats * unit)) * unit
    padded = jnp.pad(stacked, ((0, 2 * halves * lats * piece - rows), (0, 0))).astype(SEND)
    parts = padded.reshape(2, halves, lats, piece, width)
    counts = [1, halves - 1, lats - 1, lats - 1, halves - 1, 1]
    out = pl.pallas_call(
        functools.partial(reduce_kernel, lats, halves),
        out_shape=jax.ShapeDtypeStruct(parts.shape, jnp.bfloat16),
        in_specs=[pl.BlockSpec(memory_space=pltpu.VMEM)],
        out_specs=pl.BlockSpec(memory_space=pltpu.VMEM),
        scratch_shapes=[
            pltpu.VMEM((halves, lats, piece, width), SEND),
            pltpu.VMEM((halves, lats, piece, width), SEND),
            pltpu.VMEM((halves - 1, lats, piece, width), SEND),
            pltpu.VMEM((lats, piece, width), SEND),
            pltpu.VMEM((lats - 1, piece, width), SEND),
        ]
        + [pltpu.SemaphoreType.DMA((count,)) for count in counts for _ in range(2)],
        compiler_params=pltpu.CompilerParams(collective_id=0, has_side_effects=True),
    )(parts)
    return out.reshape(-1, width)[:rows]


def columns(padded, height, width, flip):
    taps = []
    for row_tap in range(3):
        for col_tap in range(3):
            top = 2 - row_tap if flip else row_tap
            side = 2 - col_tap if flip else col_tap
            taps.append(padded[:, top : top + height, side : side + width])
    return jnp.stack(taps).reshape(9 * padded.shape[0], height * width)


def dot(left, right, dims):
    return lax.dot_general(left, right, (dims, ((), ())), preferred_element_type=jnp.float32)


def on_device(fields, enc_kernel, gen_kernel, recon_grad):
    in_count, height, width = fields.shape
    hid_count = enc_kernel.shape[2]
    deep = -(-in_count // 8) * 8
    extra = deep - in_count
    lat_index = lax.axis_index("lat")
    lat_count = lax.axis_size("lat")
    lon_count = lax.axis_size("lon")
    room = jnp.zeros((extra, height, width), fields.dtype)
    plain_pair, pole_pair = face_pad(jnp.concatenate([fields, room, recon_grad, room], axis=0))
    padded_in = with_poles(plain_pair[:deep], pole_pair[:deep])
    plain_cot = plain_pair[deep:]
    pole_cot = pole_pair[deep:]
    enc_flat = jnp.pad(enc_kernel, ((0, 0), (0, 0), (0, 0), (0, extra)))
    enc_flat = enc_flat.transpose(0, 1, 3, 2).reshape(9 * deep, hid_count)
    gen_taps = jnp.pad(gen_kernel, ((0, 0), (0, 0), (0, extra), (0, 0)))
    gen_flat = gen_taps.reshape(9 * deep, hid_count)

    in_cols = columns(padded_in, height, width, False)
    pre_act = dot(enc_flat, in_cols, ((0,), (0,)))
    hidden = jax.nn.silu(pre_act).astype(jnp.bfloat16)
    plain_hid, pole_hid = face_pad(hidden.reshape(hid_count, height, width))
    padded_hid = with_poles(plain_hid, pole_hid)

    cot_cols = columns(plain_cot, height, width, True)
    upper = jnp.where(lat_index == 0, pole_cot[:, 0], 0)
    lower = jnp.where(lat_index == lat_count - 1, pole_cot[:, 1], 0)
    upper_cols = jnp.concatenate([upper[:, 2 - b : 2 - b + width] for b in range(3)], axis=0)
    lower_cols = jnp.concatenate([lower[:, 2 - b : 2 - b + width] for b in range(3)], axis=0)
    band = 3 * deep
    feat_f32 = dot(gen_flat, cot_cols, ((0,), (0,)))
    upper_term = dot(gen_flat[:band], upper_cols, ((0,), (0,)))
    lower_term = dot(gen_flat[2 * band :], lower_cols, ((0,), (0,)))
    gap = jnp.zeros((hid_count, (height - 2) * width), jnp.float32)
    feat_f32 = feat_f32 + jnp.concatenate([upper_term, gap, lower_term], axis=1)
    feat_grad = feat_f32.astype(jnp.bfloat16)
    logistic = jax.nn.sigmoid(pre_act)
    pre_grad = (
        feat_grad.astype(jnp.float32) * logistic * (1.0 + pre_act * (1.0 - logistic))
    ).astype(jnp.bfloat16)

    gen_part = dot(cot_cols, hidden, ((1,), (1,)))
    gen_upper = dot(upper_cols, hidden[:, :width], ((1,), (1,)))
    gen_lower = dot(lower_cols, hidden[:, -width:], ((1,), (1,)))
    gen_part = gen_part + jnp.concatenate(
        [gen_upper, jnp.zeros((band, hid_count), jnp.float32), gen_lower], axis=0
    )
    enc_part = dot(in_cols, pre_grad, ((1,), (1,)))
    summed = reduce_all(jnp.concatenate([enc_part, gen_part], axis=0))
    norm_scale = 1.0 / jnp.sqrt(jnp.float32(height * lat_count * width * lon_count))
    summed = summed.reshape(2, 3, 3, deep, hid_count)[:, :, :, :in_count].astype(jnp.float32) * norm_scale

    spread = dot(gen_flat, padded_hid.reshape(hid_count, -1), ((1,), (0,)))
    spread = spread.reshape(3, 3, deep, height + 2, width + 2)
    rebuilt = None
    for row_tap in range(3):
        for col_tap in range(3):
            term = spread[
                row_tap, col_tap, :in_count, row_tap : row_tap + height, col_tap : col_tap + width
            ]
            rebuilt = term if rebuilt is None else rebuilt + term
    return (
        rebuilt.astype(jnp.bfloat16),
        feat_grad.reshape(hid_count, height, width),
        summed[0].transpose(0, 1, 3, 2),
        summed[1],
    )


def solution(mesh):
    return jax.shard_map(
        on_device,
        mesh=mesh,
        in_specs=(P(None, "lat", "lon"), P(), P(), P(None, "lat", "lon")),
        out_specs=(P(None, "lat", "lon"), P(None, "lat", "lon"), P(), P()),
        check_vma=False,
    )
```

time: 220 us -> 134 us (0.61)
  waiting for transfers between devices: 131 us -> 9.92 us
  Pallas kernels: 0 us -> 43.3 us
  local copies, waits for them, and re-layouts: 13.7 us -> 31.5 us
  matrix products: 30 us -> 12.3 us
  between operations: 15 us -> 0.97 us
  other arithmetic: 11.7 us -> 21.1 us
  starting transfers between devices: 18.1 us -> 14.2 us
    psum x1 -> x0, waiting for transfers between devices: 125 us -> none  [sum_grads(): summed = lax.psum((enc_part, gen_part), ('lat', 'lon'))]
    pallas_call x0 -> x1, Pallas kernels: none -> 43.3 us  [reduce_all(): pl.pallas_call(functools.partial(reduce_kernel, lats, halves), out_shape=...]
    dot_general x51 -> x9, matrix products: 30 us -> 12.3 us  [dot(): lax.dot_general(left, right, (dims, ((), ())), preferred_element_type=jnp...]
    another operation x0 -> x3, local copies, waits for them, and re-layouts: none -> 12.3 us  [columns(): return jnp.stack(taps).reshape(9 * padded.shape[0], height * width)]
    unnamed x0 -> x8, other arithmetic: none -> 10.9 us
    unnamed x58 -> x26, local copies, waits for them, and re-layouts: 6.96 us -> 13.4 us
    mul x2 -> x1, other arithmetic: 3.94 us -> 0.1 us  [on_device(): summed.reshape(2, 3, 3, deep, hid_count)[:, :, :, :in_count]]
    slice x18 -> x3, local copies, waits for them, and re-layouts: 4.28 us -> 1.19 us  [the longest x1 1.13 us: reduce_all(): return out.reshape(-1, width)[:rows]]
  transfers between devices with their start and end apart: 11 -> 10, of which waited for: 4 -> 6; matrix products, arithmetic and copies ran while one was open for 10% -> 12% of each run, Pallas kernels for 0% -> 0%
where the time goes in v1:
time: 134 us; the launch traced here: 133 us
  Pallas kernels  43.3 us (32%)
  local copies, waits for them, and re-layouts  31.5 us (24%)
  other arithmetic  21.1 us (16%)
  starting transfers between devices  14.2 us (11%)
  matrix products  12.3 us (9%)
  waiting for transfers between devices  9.92 us (7%)
    pallas_call x1, Pallas kernels, reduce_all(): pl.pallas_call(functools.partial(reduce_kernel, lats, halves), out_shape=...  43.3 us
    unnamed x26, local copies, waits for them, and re-layouts  13.4 us
    another operation x3, local copies, waits for them, and re-layouts, columns(): return jnp.stack(taps).reshape(9 * padded.shape[0], height * width)  12.3 us
    dot_general x9, matrix products, dot(): lax.dot_general(left, right, (dims, ((), ())), preferred_element_type=jnp...  12.3 us
    unnamed x8, other arithmetic  10.9 us
    ppermute x4, starting transfers between devices, extended(): lax.ppermute(tail, axis, [(i, (i + 1) % count) for i in range(ends)])  6.58 us
    ppermute x4, starting transfers between devices, extended(): lax.ppermute(head, axis, [((i + 1) % count, i) for i in range(ends)])  6.42 us
    ppermute x4, waiting for transfers between devices, extended(): lax.ppermute(head, axis, [((i + 1) % count, i) for i in range(ends)])  6.01 us
  transfers between devices with their start and end apart: 10, of which 6 were waited for; matrix products, arithmetic and copies ran while one was open for 12% of the time, Pallas kernels for 0%

profile of v1, /device:TPU:0, one launch (start us, length us, event | category | flops | bytes accessed | tf_op | source)
XLA Modules:
  0.0 133.2 jit_solution(10416855216459290495)
XLA Ops:
  0.7 1.4 %copy.22 = bf16[69,16,128]{0,2,1:T(8,128)(2,1)S(1)} copy(bf16[69,16,128]{2,1,0:T(8,128)(2,1)} %param.4) | data formatting | bytes 565248 | tf_op args[0]
  2.1 1.3 %copy.23 = bf16[69,16,128]{0,2,1:T(8,128)(2,1)S(1)} copy(bf16[69,16,128]{2,1,0:T(8,128)(2,1)} %param.7) | data formatting | bytes 565248 | tf_op args[3]
  3.7 2.5 %collective-permute-start.1 = (bf16[144,16,1]{0,2,1:T(2,128)(2,1)S(1)}, bf16[144,16,1]{0,2,1:T(2,128)(2,1)S(1)}, u32[]{:S(2)}, u32[]{:S(2)}) collective-permute-start(bf16[144,16,1]{0,2,1:T(2,128)(2,1)S(1)} %get-tuple-element.23), channel_id=1, source_target_pairs={{1,0},{2,1},{3,2},{0,3},{5,4},{6,5},{7,6},{4,7},{9,8},{10,9},{11,1... | collective-permute-start | bytes 13832 | tf_op jit(solution)/shard_map/ppermute | solution.py:24
  6.2 0.8 pad.15
  7.6 1.7 %collective-permute-done = bf16[144,16,1]{0,2,1:T(2,128)(2,1)S(1)} collective-permute-done((bf16[144,16,1]{0,2,1:T(2,128)(2,1)S(1)}, bf16[144,16,1]{0,2,1:T(2,128)(2,1)S(1)}, u32[]{:S(2)}, u32[]{:S(2)}) %collective-permute-start) | collective-permute-done | bytes 4640 | tf_op jit(solution)/shard_map/ppermute | solution.py:22
  9.5 3.4 %collective-permute-start.3 = (bf16[144,1,130]{0,2,1:T(8,128)(2,1)S(1)}, bf16[144,1,130]{0,2,1:T(8,128)(2,1)S(1)}, u32[]{:S(2)}, u32[]{:S(2)}) collective-permute-start(bf16[144,1,130]{0,2,1:T(8,128)(2,1)S(1)} %get-tuple-element.19), channel_id=1, source_target_pairs={{0,4},{4,8},{8,12},{12,16},{16,20},{20,24},{24,28},{1,5},{5,9},{9,... | collective-permute-start | bytes 112328 | tf_op jit(solution)/shard_map/ppermute | solution.py:22
  13.0 1.3 collective-permute-start.4
  14.3 0.8 collective-permute-start.2
  15.1 0.7 pad_maximum_fusion.6
  15.8 3.3 %collective-permute-done.4 = bf16[144,1,130]{0,2,1:T(8,128)(2,1)S(1)} collective-permute-done((bf16[144,1,130]{0,2,1:T(8,128)(2,1)S(1)}, bf16[144,1,130]{0,2,1:T(8,128)(2,1)S(1)}, u32[]{:S(2)}, u32[]{:S(2)}) %collective-permute-start.4) | collective-permute-done | bytes 37472 | tf_op jit(solution)/shard_map/ppermute | solution.py:24
  19.2 5.1 %maximum_maximum_fusion = (bf16[144,17,130]{0,2,1:T(8,128)(2,1)S(1)}, bf16[144,17,130]{0,2,1:T(8,128)(2,1)S(1)}) fusion(bf16[144,16,1]{0,2,1:T(2,128)(2,1)S(1)} %collective-permute-done.1, bf16[3,16,128]{0,2,1:T(8,128)(2,1)S(1)} %broadcast_in_dim.14, bf16[69,16,128]{0,2,1:T(8,128)(2,1)S(1)} %copy.23, bf16[69,16,128]{0,2,1:T(8,128)(2,1)S(1)} %copy.22, ...), kind=kLoop, calls=%fused_computation.24 | loop fusion | flops 8910720 | bytes 1934592 | tf_op jit(solution)/shard_map/concatenate | solution.py:20
  24.3 1.2 fusion.54
  25.5 1.3 fusion.53
  26.8 1.0 fusion.52
  27.8 1.8 %fusion.48 = bf16[9,72,16,128]{1,3,2,0:T(8,128)(2,1)} fusion(bf16[9,72,16,128]{1,3,2,0:T(8,128)(2,1)} %fusion.52, bf16[3,16,128]{0,2,1:T(8,128)(2,1)S(1)} %broadcast_in_dim.14, bf16[144,16,1]{0,2,1:T(2,128)(2,1)S(1)} %collective-permute-done.1, bf16[69,16,128]{0,2,1:T(8,128)(2,1)S(1)} %copy.23, bf16[69,16,128]{0,2,1:T(8,128)(2,1)S(1)} %copy.22), kind=kLoop, calls=%fused_computation.81 | loop fusion | flops 1474560 | bytes 1106432
  29.6 0.9 bitcast_dynamic-update-slice_fusion
  30.7 1.0 fusion.32
  31.6 1.0 fusion.29
  32.6 1.0 fusion.58
  33.6 2.6 %fusion.40 = (bf16[9,72,16,128]{1,3,2,0:T(8,128)(2,1)}, bf16[9,72,16,128]{1,3,2,0:T(8,128)(2,1)}) fusion(bf16[9,72,16,128]{1,3,2,0:T(8,128)(2,1)} %bitcast_dynamic-update-slice_fusion, bf16[3,16,128]{0,2,1:T(8,128)(2,1)S(1)} %broadcast_in_dim.14, bf16[144,16,1]{0,2,1:T(2,128)(2,1)S(1)} %collective-permute-done, bf16[69,16,128]{0,2,1:T(8,128)(2,1)S(1)} %copy.23, ...), kind=kLoop, calls=%fused_computation.73 | loop fusion | flops 2801664 | bytes 1630720
  36.1 1.5 %fusion.51 = (bf16[9,72,16,128]{1,3,2,0:T(8,128)(2,1)}, bf16[9,72,16,128]{1,3,2,0:T(8,128)(2,1)}) fusion(bf16[9,72,16,128]{1,3,2,0:T(8,128)(2,1)} %get-tuple-element.20, bf16[144,17,130]{0,2,1:T(8,128)(2,1)S(1)} %get-tuple-element.16, bf16[9,72,16,128]{1,3,2,0:T(8,128)(2,1)} %get-tuple-element.21, bf16[69,16,128]{0,2,1:T(8,128)(2,1)S(1)} %copy.22), kind=kLoop, calls=%fused_computation.87 | loop fusion | bytes 1626112
  37.6 1.3 fusion.50
  38.9 1.0 fusion.49
  39.9 6.3 %copy.30 = bf16[9,72,16,128]{3,2,1,0:T(8,128)(2,1)} copy(bf16[9,72,16,128]{1,3,2,0:T(8,128)(2,1)} %fusion.49) | data formatting | bytes 5308416 | tf_op jit(solution)/shard_map/stack | solution.py:158
  46.2 1.5 %fusion.45 = bf16[9,72,16,128]{1,3,2,0:T(8,128)(2,1)} fusion(bf16[9,72,16,128]{1,3,2,0:T(8,128)(2,1)} %get-tuple-element.50, bf16[3,16,128]{0,2,1:T(8,128)(2,1)S(1)} %broadcast_in_dim.14, bf16[144,16,1]{0,2,1:T(2,128)(2,1)S(1)} %collective-permute-done.1, bf16[69,16,128]{0,2,1:T(8,128)(2,1)S(1)} %copy.23, bf16[69,16,128]{0,2,1:T(8,128)(2,1)S(1)} %copy.22), kind=kLoop, calls=%fused_computation.78 | loop fusion | flops 1474560 | bytes 1106432
  47.7 1.0 fusion.26
  48.7 1.1 fusion.23
  49.8 1.0 fusion.56
  50.7 5.0 %copy.25 = bf16[9,72,16,128]{3,2,1,0:T(8,128)(2,1)S(1)} copy(bf16[9,72,16,128]{1,3,2,0:T(8,128)(2,1)} %fusion.56) | data formatting | bytes 5308416 | tf_op jit(solution)/shard_map/stack | solution.py:158
  55.7 4.1 %multiply_convert_fusion.1 = (bf16[256,2048]{1,0:T(8,128)(2,1)}, f32[256,2048]{1,0:T(8,128)}) fusion(bf16[648,256]{1,0:T(8,128)(2,1)} %bitcast.144, bf16[81,8,16,128]{3,2,1,0:T(8,128)(2,1)S(1)} %bitcast.136), kind=kOutput, calls=%fused_computation.14 | convolution fusion | flops 682098688 | bytes 6131712 | tf_op jit(solution)/shard_map/dot_general | solution.py:162
  59.9 1.8 %copy.38 = bf16[256,2048]{0,1:T(8,128)(2,1)S(1)} copy(bf16[256,2048]{1,0:T(8,128)(2,1)} %get-tuple-element.44) | data formatting | bytes 2097152 | tf_op jit(solution)/shard_map/reshape | solution.py:186
  62.9 2.9 %fusion.7 = bf16[256,2048]{1,0:T(8,128)(2,1)S(1)} fusion(bf16[648,256]{1,0:T(8,128)(2,1)S(1)} %bitcast.143, bf16[81,8,16,128]{3,2,1,0:T(8,128)(2,1)} %bitcast.134, f32[256,128]{1,0:T(8,128)S(1)} %fusion.67, f32[256,128]{1,0:T(8,128)S(1)} %fusion.68, f32[2048]{0:T(1024)S(1)} %pad.23.clone), kind=kOutput, calls=%fused_computation.8 | convolution fusion | flops 681574400 | bytes 4304896 | tf_op jit(solution)/shard_map/dot_general | solution.py:162
  66.0 1.4 %fusion.3 = f32[648,256]{1,0:T(8,128)S(1)} fusion(bf16[81,8,16,128]{3,2,1,0:T(8,128)(2,1)S(1)} %bitcast.137, f32[256,2048]{1,0:T(8,128)S(1)} %copy-done.7, bf16[256,2048]{1,0:T(8,128)(2,1)S(1)} %fusion.7), kind=kOutput, calls=%fused_computation.4 | convolution fusion | flops 684720128 | bytes 6463488 | tf_op jit(solution)/shard_map/dot_general | solution.py:162
  67.8 0.9 fusion.14
  68.7 1.3 select_maximum_fusion
  70.0 43.3 %shard_map.75 = bf16[2,2,8,48,256]{4,3,2,1,0:T(8,128)(2,1)} custom-call(f32[2,2,8,48,256]{4,3,2,1,0:T(8,128)} %bitcast.131), custom_call_target="tpu_custom_call" | custom-call | tf_op jit(solution)/shard_map/pallas_call | solution.py:133
  113.3 1.1 slice.328
  114.9 1.4 %collective-permute-start.6 = (bf16[256,16,1]{0,2,1:T(2,128)(2,1)S(1)}, bf16[256,16,1]{0,2,1:T(2,128)(2,1)S(1)}, u32[]{:S(2)}, u32[]{:S(2)}) collective-permute-start(bf16[256,16,1]{0,2,1:T(2,128)(2,1)S(1)} %get-tuple-element.29), channel_id=1, source_target_pairs={{1,0},{2,1},{3,2},{0,3},{5,4},{6,5},{7,6},{4,7},{9,8},{10,9},{11,1... | collective-permute-start | bytes 24584 | tf_op jit(solution)/shard_map/ppermute | solution.py:24
  116.4 1.3 collective-permute-done.5
  117.8 2.7 %collective-permute-start.8 = (bf16[256,1,130]{0,2,1:T(8,128)(2,1)S(1)}, bf16[256,1,130]{0,2,1:T(8,128)(2,1)S(1)}, u32[]{:S(2)}, u32[]{:S(2)}) collective-permute-start(bf16[256,1,130]{0,2,1:T(8,128)(2,1)S(1)} %get-tuple-element.26), channel_id=1, source_target_pairs={{0,4},{4,8},{8,12},{12,16},{16,20},{20,24},{24,28},{1,5},{5,9},{9,... | collective-permute-start | bytes 199688 | tf_op jit(solution)/shard_map/ppermute | solution.py:22
  120.5 1.3 collective-permute-start.9
  122.2 1.2 slice_bitcast_fusion
  123.4 1.2 copy.41
  124.6 2.1 %collective-permute-done.9 = bf16[256,1,130]{0,2,1:T(8,128)(2,1)S(1)} collective-permute-done((bf16[256,1,130]{0,2,1:T(8,128)(2,1)S(1)}, bf16[256,1,130]{0,2,1:T(8,128)(2,1)S(1)}, u32[]{:S(2)}, u32[]{:S(2)}) %collective-permute-start.9) | collective-permute-done | bytes 66592 | tf_op jit(solution)/shard_map/ppermute | solution.py:24
  126.7 0.9 collective-permute-done.7
  129.6 1.8 %fusion.17 = f32[3,3,72,18,130]{2,4,3,1,0:T(8,128)S(1)} fusion(bf16[18,130,256,1,1]{2,1,0,3,4:T(8,128)(2,1)S(1)} %reshape.70, bf16[3,3,69,256]{3,2,1,0:T(8,128)(2,1)S(1)} %copy-done.1), kind=kOutput, calls=%fused_computation.21 | convolution fusion | flops 776355840 | bytes 7581312 | tf_op jit(solution)/shard_map/dot_general | solution.py:162
  131.4 0.8 fusion.59
  132.2 1.0 copy.33
  (48 shorter events, 6.0 us)
Async XLA Ops:
  0.6 5.5 %copy-start = (bf16[3,3,69,256]{3,2,1,0:T(8,128)(2,1)S(1)}, bf16[3,3,69,256]{3,2,1,0:T(8,128)(2,1)}, u32[]{:S(2)}) copy-start(bf16[3,3,69,256]{3,2,1,0:T(8,128)(2,1)} %param.6) | copy-start | bytes 953860
  0.6 5.6 %copy-start.6 = (bf16[3,3,256,69]{2,3,1,0:T(8,128)(2,1)S(1)}, bf16[3,3,256,69]{2,3,1,0:T(8,128)(2,1)}, u32[]{:S(2)}) copy-start(bf16[3,3,256,69]{2,3,1,0:T(8,128)(2,1)} %param.5) | copy-start | bytes 953860
  3.7 3.9 %collective-permute-start.1 = (bf16[144,16,1]{0,2,1:T(2,128)(2,1)S(1)}, bf16[144,16,1]{0,2,1:T(2,128)(2,1)S(1)}, u32[]{:S(2)}, u32[]{:S(2)}) collective-permute-start(bf16[144,16,1]{0,2,1:T(2,128)(2,1)S(1)} %get-tuple-element.23), channel_id=1, source_target_pairs={{1,0},{2,1},{3,2},{0,3},{5,4},{6,5},{7,6},{4,7},{9,8},{10,9},{11,1... | collective-permute-start | bytes 13832 | tf_op jit(solution)/shard_map/ppermute | solution.py:24
  6.1 3.2 %collective-permute-start = (bf16[144,16,1]{0,2,1:T(2,128)(2,1)S(1)}, bf16[144,16,1]{0,2,1:T(2,128)(2,1)S(1)}, u32[]{:S(2)}, u32[]{:S(2)}) collective-permute-start(bf16[144,16,1]{0,2,1:T(2,128)(2,1)S(1)} %get-tuple-element.22), channel_id=1, source_target_pairs={{0,1},{1,2},{2,3},{3,0},{4,5},{5,6},{6,7},{7,4},{8,9},{9,10},{10,1... | collective-permute-start | bytes 13832 | tf_op jit(solution)/shard_map/ppermute | solution.py:22
  9.5 6.3 %collective-permute-start.3 = (bf16[144,1,130]{0,2,1:T(8,128)(2,1)S(1)}, bf16[144,1,130]{0,2,1:T(8,128)(2,1)S(1)}, u32[]{:S(2)}, u32[]{:S(2)}) collective-permute-start(bf16[144,1,130]{0,2,1:T(8,128)(2,1)S(1)} %get-tuple-element.19), channel_id=1, source_target_pairs={{0,4},{4,8},{8,12},{12,16},{16,20},{20,24},{24,28},{1,5},{5,9},{9,... | collective-permute-start | bytes 112328 | tf_op jit(solution)/shard_map/ppermute | solution.py:22
  13.0 6.2 %collective-permute-start.4 = (bf16[144,1,130]{0,2,1:T(8,128)(2,1)S(1)}, bf16[144,1,130]{0,2,1:T(8,128)(2,1)S(1)}, u32[]{:S(2)}, u32[]{:S(2)}) collective-permute-start(bf16[144,1,130]{0,2,1:T(8,128)(2,1)S(1)} %get-tuple-element.18), channel_id=1, source_target_pairs={{4,0},{8,4},{12,8},{16,12},{20,16},{24,20},{28,24},{5,1},{9,5},{13... | collective-permute-start | bytes 112328 | tf_op jit(solution)/shard_map/ppermute | solution.py:24
  14.3 16.3 %collective-permute-start.2 = (bf16[144,2,130]{0,2,1:T(8,128)(2,1)S(1)}, bf16[144,2,130]{0,2,1:T(8,128)(2,1)S(1)}, u32[]{:S(2)}, u32[]{:S(2)}) collective-permute-start(bf16[144,2,130]{0,2,1:T(8,128)(2,1)S(1)} %pad_maximum_fusion.17), channel_id=1, source_target_pairs={{0,2},{1,3},{2,0},{3,1},{4,6},{5,7},{6,4},{7,5},{8,10},{9,11},{10,... | collective-permute-start | bytes 224648 | tf_op jit(solution)/shard_map/ppermute | solution.py:34
  55.7 4.1 %copy-start.3 = (bf16[9,72,16,128]{3,2,1,0:T(8,128)(2,1)}, bf16[9,72,16,128]{3,2,1,0:T(8,128)(2,1)S(1)}, u32[]{:S(2)}) copy-start(bf16[9,72,16,128]{3,2,1,0:T(8,128)(2,1)S(1)} %copy.25) | copy-start | bytes 7962628
  59.9 1.8 %copy-start.5 = (bf16[256,2048]{1,0:T(8,128)(2,1)S(1)}, bf16[256,2048]{1,0:T(8,128)(2,1)}, u32[]{:S(2)}) copy-start(bf16[256,2048]{1,0:T(8,128)(2,1)} %get-tuple-element.44) | copy-start | bytes 3145732
  62.8 2.9 %copy-start.4 = (bf16[9,72,16,128]{3,2,1,0:T(8,128)(2,1)S(1)}, bf16[9,72,16,128]{3,2,1,0:T(8,128)(2,1)}, u32[]{:S(2)}) copy-start(bf16[9,72,16,128]{3,2,1,0:T(8,128)(2,1)} %copy-done.3) | copy-start | bytes 7962628
  62.9 3.2 %copy-start.7 = (f32[256,2048]{1,0:T(8,128)S(1)}, f32[256,2048]{1,0:T(8,128)}, u32[]{:S(2)}) copy-start(f32[256,2048]{1,0:T(8,128)} %get-tuple-element.45) | copy-start | bytes 6291460
  66.0 1.7 %copy-start.2 = (bf16[9,72,16,128]{3,2,1,0:T(8,128)(2,1)S(1)}, bf16[9,72,16,128]{3,2,1,0:T(8,128)(2,1)}, u32[]{:S(2)}) copy-start(bf16[9,72,16,128]{3,2,1,0:T(8,128)(2,1)} %copy.30) | copy-start | bytes 7962628
  114.5 3.2 %collective-permute-start.5 = (bf16[256,16,1]{0,2,1:T(2,128)(2,1)S(1)}, bf16[256,16,1]{0,2,1:T(2,128)(2,1)S(1)}, u32[]{:S(2)}, u32[]{:S(2)}) collective-permute-start(bf16[256,16,1]{0,2,1:T(2,128)(2,1)S(1)} %get-tuple-element.28), channel_id=1, source_target_pairs={{0,1},{1,2},{2,3},{3,0},{4,5},{5,6},{6,7},{7,4},{8,9},{9,10},{10,1... | collective-permute-start | bytes 24584 | tf_op jit(solution)/shard_map/ppermute | solution.py:22
  114.9 2.8 %collective-permute-start.6 = (bf16[256,16,1]{0,2,1:T(2,128)(2,1)S(1)}, bf16[256,16,1]{0,2,1:T(2,128)(2,1)S(1)}, u32[]{:S(2)}, u32[]{:S(2)}) collective-permute-start(bf16[256,16,1]{0,2,1:T(2,128)(2,1)S(1)} %get-tuple-element.29), channel_id=1, source_target_pairs={{1,0},{2,1},{3,2},{0,3},{5,4},{6,5},{7,6},{4,7},{9,8},{10,9},{11,1... | collective-permute-start | bytes 24584 | tf_op jit(solution)/shard_map/ppermute | solution.py:24
  117.8 6.8 %collective-permute-start.8 = (bf16[256,1,130]{0,2,1:T(8,128)(2,1)S(1)}, bf16[256,1,130]{0,2,1:T(8,128)(2,1)S(1)}, u32[]{:S(2)}, u32[]{:S(2)}) collective-permute-start(bf16[256,1,130]{0,2,1:T(8,128)(2,1)S(1)} %get-tuple-element.26), channel_id=1, source_target_pairs={{0,4},{4,8},{8,12},{12,16},{16,20},{20,24},{24,28},{1,5},{5,9},{9,... | collective-permute-start | bytes 199688 | tf_op jit(solution)/shard_map/ppermute | solution.py:22
  120.5 6.2 %collective-permute-start.9 = (bf16[256,1,130]{0,2,1:T(8,128)(2,1)S(1)}, bf16[256,1,130]{0,2,1:T(8,128)(2,1)S(1)}, u32[]{:S(2)}, u32[]{:S(2)}) collective-permute-start(bf16[256,1,130]{0,2,1:T(8,128)(2,1)S(1)} %get-tuple-element.27), channel_id=1, source_target_pairs={{4,0},{8,4},{12,8},{16,12},{20,16},{24,20},{28,24},{5,1},{9,5},{13... | collective-permute-start | bytes 199688 | tf_op jit(solution)/shard_map/ppermute | solution.py:24
  121.8 5.8 %collective-permute-start.7 = (bf16[256,2,130]{0,2,1:T(8,128)(2,1)S(1)}, bf16[256,2,130]{0,2,1:T(8,128)(2,1)S(1)}, u32[]{:S(2)}, u32[]{:S(2)}) collective-permute-start(bf16[256,2,130]{0,2,1:T(8,128)(2,1)S(1)} %pad_maximum_fusion.18), channel_id=1, source_target_pairs={{0,2},{1,3},{2,0},{3,1},{4,6},{5,7},{6,4},{7,5},{8,10},{9,11},{10,... | collective-permute-start | bytes 399368 | tf_op jit(solution)/shard_map/ppermute | solution.py:34
  128.6 1.0 copy-start.1

commit v2 on v1

v2 whole, which is shorter than its diff:
```python
import functools

import jax
import jax.numpy as jnp
from jax import lax
from jax.experimental import pallas as pl
from jax.experimental.pallas import tpu as pltpu
from jax.sharding import PartitionSpec as P

MESH = pl.DeviceIdType.MESH
SEND = jnp.float32
F32 = jnp.float32
BF16 = jnp.bfloat16


def dot(left, right, dims):
    return lax.dot_general(left, right, (dims, ((), ())), preferred_element_type=F32)


def shifted(value, amount):
    return pltpu.roll(value, amount, 1)


def pack_columns(load, out_ref, count, group, height, width):
    lane = lax.broadcasted_iota(jnp.int32, (group, width), 1)
    for start in range(0, count, group):
        first = jnp.zeros((group, width), F32)
        last = jnp.zeros((group, width), F32)
        for row in range(height):
            cells = load(row, start, group).astype(F32)
            first = jnp.where(lane == row, shifted(cells, row) if row else cells, first)
            last = jnp.where(lane == row, shifted(cells, row + 1), last)
        out_ref[0, start : start + group] = first.astype(BF16)
        out_ref[1, start : start + group] = last.astype(BF16)


def widen_row(load, halo_ref, row, start, group, width):
    lane = lax.broadcasted_iota(jnp.int32, (group, width), 1)
    cells = load(row, start, group)
    wide = cells.astype(F32)
    left = shifted(halo_ref[0, start : start + group].astype(F32), lax.rem(width - row, width))
    right = shifted(halo_ref[1, start : start + group].astype(F32), width - 1 - row)
    before = jnp.where(lane == 0, left, shifted(wide, 1)).astype(BF16)
    after = jnp.where(lane == width - 1, right, shifted(wide, width - 1)).astype(BF16)
    return before, cells, after


def layer_kernel(
    lats, halves, deep, wide_deep, in_ref, we_ref, wf_ref, wr_ref, reb_ref, feat_ref, grad_ref,
    xg, hs, hrow, packed, arrived, hpacked, harrived, accx, accg, parts,
    from_pair, held_pair, from_lon, held_lon, from_lat, *sems,
):
    height, both, width = in_ref.shape
    hid = hrow.shape[1]
    lons = 2 * halves
    band = 3 * wide_deep
    lat = lax.axis_index("lat")
    lon = lax.axis_index("lon")
    half = lax.div(lon, 2)
    core = lax.rem(lon, 2)
    other = 1 - core
    below_top = lax.div(lat + lats - 1, lats)
    above_end = lax.div(2 * lats - 2 - lat, lats)

    def lon_peer(step):
        return (lat, lax.rem(half + step, halves) * 2 + core)

    def lat_peer(step):
        return (lax.rem(lat + step, lats), lon)

    pair = (lat, half * 2 + other)
    outer = (lat, lax.rem(lon + lons + 2 * core - 1, lons))
    west = (lat, lax.rem(lon + lons - 1, lons))
    east = (lat, lax.rem(lon + 1, lons))
    north = (lat - below_top, lax.rem(lon + (1 - below_top) * halves, lons))
    south = (lat + above_end, lax.rem(lon + (1 - above_end) * halves, lons))

    barrier = pltpu.get_barrier_semaphore()
    peers = [pair, outer]
    peers += [lon_peer(step) for step in range(1, halves)]
    peers += [lat_peer(step) for step in range(1, lats)]
    for peer in peers:
        pl.semaphore_signal(barrier, inc=1, device_id=peer, device_id_type=MESH)
    pl.semaphore_wait(barrier, len(peers))

    def send(src, dst, phase, send_slot, recv_slot, peer):
        copy = pltpu.make_async_remote_copy(
            src_ref=src,
            dst_ref=dst,
            send_sem=sems[2 * phase].at[send_slot],
            recv_sem=sems[2 * phase + 1].at[recv_slot],
            device_id=peer,
            device_id_type=MESH,
        )
        copy.start()
        return copy

    def swap_columns(source, target, phase):
        return [
            send(source.at[1], target.at[0], phase, 0, 0, east),
            send(source.at[0], target.at[1], phase, 1, 1, west),
        ]

    def swap_rows(rows, phase):
        return [
            send(rows.at[1], rows.at[below_top * (height + 1)], phase, 0, below_top, north),
            send(rows.at[height], rows.at[(1 - above_end) * (height + 1)], phase, 1, 1 - above_end, south),
        ]

    def wait_rows(copies, rows, phase):
        for copy in copies:
            copy.wait_send()
        for slot in range(2):
            edge = rows.at[slot * (height + 1)]
            pltpu.make_async_copy(edge, edge, sems[2 * phase + 1].at[slot]).wait()

    def load_in(row, start, group):
        return in_ref[row, start : start + group]

    pack_columns(load_in, packed, both, both // 2, height, width)
    copies = swap_columns(packed, arrived, 6)
    accx[...] = jnp.zeros_like(accx)
    accg[...] = jnp.zeros_like(accg)
    for copy in copies:
        copy.wait()

    def widen_in(row):
        before, cells, after = widen_row(load_in, arrived, row, 0, wide_deep, width)
        for place, value in enumerate((before, cells, after)):
            xg[row + 1, place * wide_deep : (place + 1) * wide_deep] = value
        before, cells, after = widen_row(load_in, arrived, row, wide_deep, wide_deep, width)
        for place, value in enumerate((after, cells, before)):
            xg[row + 1, band + place * wide_deep : band + (place + 1) * wide_deep] = value

    widen_in(0)
    widen_in(height - 1)
    copies = swap_rows(xg, 7)

    @pl.loop(1, height - 1)
    def _(row):
        widen_in(row)

    def window(ref, row, start, count):
        tall = 3 * count
        return jnp.concatenate(
            [
                ref[pl.ds(row, 3), start : start + count].reshape(tall, width),
                ref[pl.ds(row + 1, 3), start : start + count].reshape(tall, width),
            ],
            axis=1,
        )

    def cells_step(row, extra):
        in_cols = window(xg, row, 0, band)
        cot_cols = window(xg, row, band, band)
        pre_act = dot(we_ref[...], in_cols, ((1,), (0,)))
        logistic = 1.0 / (1.0 + jnp.exp(-pre_act))
        hidden = (pre_act * logistic).astype(BF16)
        hrow[row] = hidden[:, :width]
        hrow[row + 1] = hidden[:, width:]
        feat = dot(wf_ref[...], cot_cols, ((1,), (0,)))
        if extra is not None:
            feat = feat + extra
        feat = feat.astype(BF16)
        feat_ref[row] = feat[:, :width]
        feat_ref[row + 1] = feat[:, width:]
        pre_grad = (
            feat.astype(F32) * logistic * (1.0 + pre_act * (1.0 - logistic))
        ).astype(BF16)
        accg[...] += dot(cot_cols, hidden, ((1,), (1,)))
        accx[...] += dot(in_cols, pre_grad, ((1,), (1,)))

    @pl.loop(1, height // 2 - 1)
    def _(step):
        cells_step(step * 2, None)

    wait_rows(copies, xg, 7)
    open_gap = jnp.zeros((hid, width), F32)
    for slot, inside, start, row in ((0, below_top, 2 * band, 0), (1, above_end, 0, height - 2)):
        edge = xg[slot * (height + 1), band:]
        at_pole = jnp.where(inside == 0, edge, jnp.zeros_like(edge))
        xg[slot * (height + 1), band:] = jnp.where(inside == 0, jnp.zeros_like(edge), edge)
        term = dot(wf_ref[:, start : start + band], at_pole, ((1,), (0,)))
        both_terms = [term, open_gap] if slot == 0 else [open_gap, term]
        cells_step(row, jnp.concatenate(both_terms, axis=1))
        accg[start : start + band] += dot(at_pole, hrow[row + slot], ((1,), (1,)))

    def load_hid(row, start, group):
        return hrow[row, start : start + group]

    for tap in range(9):
        row_tap, col_tap = divmod(tap, 3)
        source = (2 - row_tap) * 3 + col_tap
        parts[tap * deep : (tap + 1) * deep] = accx[
            tap * wide_deep : tap * wide_deep + deep
        ].astype(SEND)
        parts[(9 + tap) * deep : (10 + tap) * deep] = accg[
            source * wide_deep : source * wide_deep + deep
        ].astype(SEND)
    used = 18 * deep
    if parts.shape[0] > used:
        parts[used:] = jnp.zeros((parts.shape[0] - used, hid), SEND)

    half_rows = parts.shape[0] // 2
    lon_rows = half_rows // halves
    lat_rows = lon_rows // lats

    def at(ref, index, count):
        return ref.at[pl.ds(pl.multiple_of(index * count, 16), count)]

    pair_copy = send(at(parts, other, half_rows), from_pair, 0, 0, 0, pair)
    pack_columns(load_hid, hpacked, hid, 64, height, width)
    column_copies = swap_columns(hpacked, harrived, 8)
    pair_copy.wait()
    held_pair[...] = (at(parts, core, half_rows)[...].astype(F32) + from_pair[...].astype(F32)).astype(SEND)
    lon_copies = []
    for step in range(1, halves):
        target = lax.rem(half + step, halves)
        lon_copies.append(
            send(at(held_pair, target, lon_rows), from_lon.at[step - 1], 1, step - 1, step - 1, lon_peer(step))
        )
    for copy in column_copies:
        copy.wait()

    def widen_hid(row):
        for start in range(0, hid, 64):
            parts_row = widen_row(load_hid, harrived, row, start, 64, width)
            for place, value in enumerate(parts_row):
                hs[row + 1, place * hid + start : place * hid + start + 64] = value

    widen_hid(0)
    widen_hid(height - 1)
    row_copies = swap_rows(hs, 9)

    @pl.loop(1, height - 1)
    def _(row):
        widen_hid(row)

    for copy in lon_copies:
        copy.wait()
    total = at(held_pair, half, lon_rows)[...].astype(F32)
    for step in range(1, halves):
        total = total + from_lon[step - 1].astype(F32)
    held_lon[...] = total.astype(SEND)
    lat_copies = []
    for step in range(1, lats):
        target = lax.rem(lat + step, lats)
        lat_copies.append(
            send(at(held_lon, target, lat_rows), from_lat.at[step - 1], 2, step - 1, step - 1, lat_peer(step))
        )

    def rebuild(row):
        value = dot(wr_ref[...], window(hs, row, 0, 3 * hid), ((1,), (0,))).astype(BF16)
        reb_ref[row] = value[:, :width]
        reb_ref[row + 1] = value[:, width:]

    @pl.loop(1, height // 2 - 1)
    def _(step):
        rebuild(step * 2)

    for copy in lat_copies:
        copy.wait()
    total = at(held_lon, lat, lat_rows)[...].astype(F32)
    for step in range(1, lats):
        total = total + from_lat[step - 1].astype(F32)
    place = (core * halves + half) * lats + lat
    mine = at(grad_ref, place, lat_rows)
    mine[...] = total.astype(grad_ref.dtype)
    copies = [send(mine, mine, 3, step - 1, step - 1, lat_peer(step)) for step in range(1, lats)]
    wait_rows(row_copies, hs, 9)
    rebuild(0)
    rebuild(height - 2)
    for copy in copies:
        copy.wait()
    mine = at(grad_ref, core * halves + half, lon_rows)
    copies = [send(mine, mine, 4, step - 1, step - 1, lon_peer(step)) for step in range(1, halves)]
    for copy in copies:
        copy.wait()
    mine = at(grad_ref, core, half_rows)
    send(mine, mine, 5, 0, 0, pair).wait()


def on_device(fields, enc_kernel, gen_kernel, recon_grad):
    in_count, height, width = fields.shape
    hid = enc_kernel.shape[2]
    deep = -(-in_count // 8) * 8
    wide_deep = -(-in_count // 16) * 16
    extra = wide_deep - in_count
    lats = lax.axis_size("lat")
    lons = lax.axis_size("lon")
    halves = lons // 2
    room = ((0, 0), (0, extra), (0, 0))
    stacked = jnp.concatenate(
        [
            jnp.pad(fields.transpose(1, 0, 2), room),
            jnp.pad(recon_grad.transpose(1, 0, 2), room),
        ],
        axis=1,
    )
    band = 3 * wide_deep
    enc_flat = jnp.pad(enc_kernel, ((0, 0), (0, 0), (0, 0), (0, extra)))
    enc_flat = enc_flat.transpose(2, 0, 1, 3).reshape(hid, 3 * band)
    gen_taps = jnp.pad(gen_kernel, ((0, 0), (0, 0), (0, extra), (0, 0)))
    back_flat = gen_taps[::-1].transpose(3, 0, 1, 2).reshape(hid, 3 * band)
    gen_flat = gen_taps.transpose(2, 0, 1, 3).reshape(wide_deep, 9 * hid)
    pieces = lons * lats
    lat_rows = -(-18 * deep // (pieces * 16)) * 16
    lon_rows = lats * lat_rows
    half_rows = halves * lon_rows
    counts = [1, halves - 1, lats - 1, lats - 1, halves - 1, 1, 2, 2, 2, 2]
    rebuilt, feat, summed = pl.pallas_call(
        functools.partial(layer_kernel, lats, halves, deep, wide_deep),
        out_shape=[
            jax.ShapeDtypeStruct((height, wide_deep, width), BF16),
            jax.ShapeDtypeStruct((height, hid, width), BF16),
            jax.ShapeDtypeStruct((2 * half_rows, hid), BF16),
        ],
        in_specs=[pl.BlockSpec(memory_space=pltpu.VMEM)] * 4,
        out_specs=[pl.BlockSpec(memory_space=pltpu.VMEM)] * 3,
        scratch_shapes=[
            pltpu.VMEM((height + 2, 2 * band, width), BF16),
            pltpu.VMEM((height + 2, 3 * hid, width), BF16),
            pltpu.VMEM((height, hid, width), BF16),
            pltpu.VMEM((2, 2 * wide_deep, width), BF16),
            pltpu.VMEM((2, 2 * wide_deep, width), BF16),
            pltpu.VMEM((2, hid, width), BF16),
            pltpu.VMEM((2, hid, width), BF16),
            pltpu.VMEM((3 * band, hid), F32),
            pltpu.VMEM((3 * band, hid), F32),
            pltpu.VMEM((2 * half_rows, hid), SEND),
            pltpu.VMEM((half_rows, hid), SEND),
            pltpu.VMEM((half_rows, hid), SEND),
            pltpu.VMEM((halves - 1, lon_rows, hid), SEND),
            pltpu.VMEM((lon_rows, hid), SEND),
            pltpu.VMEM((lats - 1, lat_rows, hid), SEND),
        ]
        + [pltpu.SemaphoreType.DMA((count,)) for count in counts for _ in range(2)],
        compiler_params=pltpu.CompilerParams(
            collective_id=0, has_side_effects=True, vmem_limit_bytes=48 << 20
        ),
    )(stacked, enc_flat, back_flat, gen_flat)
    norm_scale = 1.0 / jnp.sqrt(F32(height * lats * width * lons))
    grads = summed[: 18 * deep].reshape(2, 3, 3, deep, hid)[:, :, :, :in_count].astype(F32) * norm_scale
    return (
        rebuilt[:, :in_count].transpose(1, 0, 2),
        feat.transpose(1, 0, 2),
        grads[0].transpose(0, 1, 3, 2),
        grads[1],
    )


def solution(mesh):
    return jax.shard_map(
        on_device,
        mesh=mesh,
        in_specs=(P(None, "lat", "lon"), P(), P(), P(None, "lat", "lon")),
        out_specs=(P(None, "lat", "lon"), P(None, "lat", "lon"), P(), P()),
        check_vma=False,
    )
```

time: 134 us -> 62.3 us (0.46)
  local copies, waits for them, and re-layouts: 31.5 us -> 6.7 us
  other arithmetic: 21.1 us -> 0.15 us
  starting transfers between devices: 14.2 us -> 0 us
  matrix products: 12.3 us -> 0 us
  Pallas kernels: 43.3 us -> 54.5 us
  waiting for transfers between devices: 9.92 us -> 0 us
    ppermute x10 -> x0, starting transfers between devices: 14.2 us -> none  [the longest x4 6.58 us: extended(): lax.ppermute(tail, axis, [(i, (i + 1) % count) for i in range(ends)])]
    another operation x3 -> x0, local copies, waits for them, and re-layouts: 12.3 us -> none  [columns(): return jnp.stack(taps).reshape(9 * padded.shape[0], height * width)]
    dot_general x9 -> x0, matrix products: 12.3 us -> none  [dot(): lax.dot_general(left, right, (dims, ((), ())), preferred_element_type=jnp...]
    pallas_call x1, Pallas kernels: 43.3 us -> 54.5 us  [on_device(): pl.pallas_call(functools.partial(layer_kernel, lats, halves, deep, wide_d...]
    unnamed x8 -> x0, other arithmetic: 10.9 us -> none
    unnamed x26 -> x8, local copies, waits for them, and re-layouts: 13.4 us -> 3.15 us
    ppermute x10 -> x0, waiting for transfers between devices: 9.92 us -> none  [the longest x4 6.01 us: extended(): lax.ppermute(head, axis, [((i + 1) % count, i) for i in range(ends)])]
    concatenate x7 -> x1, other arithmetic: 7.9 us -> 0.05 us  [on_device(): jnp.concatenate([jnp.pad(fields.transpose(1, 0, 2), room), jnp.pad(recon_...]
  transfers between devices with their start and end apart: 10 -> 0, of which waited for: 6 -> 0; matrix products, arithmetic and copies ran while one was open for 12% -> 0% of each run, Pallas kernels for 0% -> 0%
where the time goes in v2:
time: 62.3 us; the launch traced here: 62.1 us
  Pallas kernels  54.5 us (87%)
  local copies, waits for them, and re-layouts  6.7 us (11%)
  between operations  0.75 us (1%)
    pallas_call x1, Pallas kernels, on_device(): pl.pallas_call(functools.partial(layer_kernel, lats, halves, deep, wide_d...  54.5 us
    unnamed x8, local copies, waits for them, and re-layouts  3.15 us

profile of v2, /device:TPU:0, one launch (start us, length us, event | category | flops | bytes accessed | tf_op | source)
XLA Modules:
  0.0 62.1 jit_solution(14629580578652857038)
XLA Ops:
  0.6 0.0 copy-start.1
  0.6 0.0 copy-start.2
  0.7 1.1 %pad.17 = bf16[3,3,256,80]{2,3,1,0:T(8,128)(2,1)S(1)} pad(bf16[3,3,256,69]{2,3,1,0:T(8,128)(2,1)} %param.5, bf16[]{:T(256)} %constant.1.clone.1), padding=0_0x0_0x0_0x0_11 | pad | bytes 686594 | tf_op jit(solution)/shard_map/jit(_pad)/pad | solution.py:301
  1.7 0.2 copy.18.we_ref
  1.9 0.0 copy-done.1
  1.9 0.0 copy-done.2
  1.9 0.0 copy-start
  1.9 0.2 copy_bitcast_fusion
  2.1 0.1 fusion.2.in_ref
  2.1 0.7 %copy-done = bf16[3,3,69,256]{3,2,1,0:T(8,128)(2,1)S(1)} copy-done((bf16[3,3,69,256]{3,2,1,0:T(8,128)(2,1)S(1)}, bf16[3,3,69,256]{3,2,1,0:T(8,128)(2,1)}, u32[]{:S(2)}) %copy-start) | copy-done | bytes 317976
  2.9 0.3 copy.17
  3.2 0.4 reshape.22.wr_ref
  3.7 0.2 copy.19.wf_ref
  3.8 54.5 %shard_map.75 = (bf16[16,80,128]{2,1,0:T(8,128)(2,1)S(1)}, bf16[16,256,128]{2,1,0:T(8,128)(2,1)S(1)}, bf16[1536,256]{1,0:T(8,128)(2,1)S(1)}) custom-call(bf16[16,160,128]{2,1,0:T(8,128)(2,1)S(1)} %fusion.2.in_ref, bf16[256,720]{1,0:T(8,128)(2,1)S(1)} %copy.18.we_ref, bf16[256,720]{1,0:T(8,128)(2,1)S(1)} %copy.19.wf_ref, bf16[80,2304]{1,0:T(8,128)(2,1)S(1)} %reshape.22.wr_ref), custom_call_target="tpu_custom_call" | custom-call | tf_op jit(solution)/shard_map/pallas_call | solution.py:311
  58.4 0.7 %copy.20 = bf16[69,16,128]{2,1,0:T(8,128)(2,1)} copy(bf16[69,16,128]{2,0,1:T(8,128)(2,1)S(1)} %slice_bitcast_fusion.2) | data formatting | bytes 565248
  59.1 1.6 %copy.21 = bf16[256,16,128]{2,1,0:T(8,128)(2,1)} copy(bf16[256,16,128]{2,0,1:T(8,128)(2,1)S(1)} %bitcast.22) | data formatting | bytes 2097152
  60.8 0.1 convert_multiply_fusion
  60.9 1.2 %slice_bitcast_fusion = (f32[3,3,69,256]{3,2,1,0:T(8,128)}, f32[3,3,256,69]{2,3,1,0:T(8,128)}) fusion(f32[2,3,3,69,256]{4,3,2,1,0:T(8,128)S(1)} %convert_multiply_fusion), kind=kLoop, calls=%fused_computation.5 | loop fusion | bytes 2543616 | tf_op jit(solution)/shard_map/squeeze | solution.py:348
  (4 shorter events, 0.1 us)
Async XLA Ops:
  0.6 1.3 %copy-start.1 = (bf16[69,16,128]{2,1,0:T(8,128)(2,1)S(1)}, bf16[69,16,128]{2,1,0:T(8,128)(2,1)}, u32[]{:S(2)}) copy-start(bf16[69,16,128]{2,1,0:T(8,128)(2,1)} %param.7) | copy-start | bytes 847876
  0.6 1.3 %copy-start.2 = (bf16[69,16,128]{2,1,0:T(8,128)(2,1)S(1)}, bf16[69,16,128]{2,1,0:T(8,128)(2,1)}, u32[]{:S(2)}) copy-start(bf16[69,16,128]{2,1,0:T(8,128)(2,1)} %param.4) | copy-start | bytes 847876
  1.9 1.0 %copy-start = (bf16[3,3,69,256]{3,2,1,0:T(8,128)(2,1)S(1)}, bf16[3,3,69,256]{3,2,1,0:T(8,128)(2,1)}, u32[]{:S(2)}) copy-start(bf16[3,3,69,256]{3,2,1,0:T(8,128)(2,1)} %param.6) | copy-start | bytes 953860

commit v3 on v2

v3 whole, which is shorter than its diff:
```python
import functools

import jax
import jax.numpy as jnp
from jax import lax
from jax.experimental import pallas as pl
from jax.experimental.pallas import tpu as pltpu
from jax.sharding import PartitionSpec as P

MESH = pl.DeviceIdType.MESH
LINK = jnp.bfloat16
F32 = jnp.float32
BF16 = jnp.bfloat16


def dot(left, right, dims):
    return lax.dot_general(left, right, (dims, ((), ())), preferred_element_type=F32)


def shifted(value, amount):
    return pltpu.roll(value, amount, 1)


def pack_columns(load, out_ref, count, group, tall, width):
    lane = lax.broadcasted_iota(jnp.int32, (group, width), 1)
    for start in range(0, count, group):
        first = jnp.zeros((group, width), F32)
        last = jnp.zeros((group, width), F32)
        for row in range(tall):
            cells = load(row, start, group).astype(F32)
            first = jnp.where(lane == row, shifted(cells, row) if row else cells, first)
            last = jnp.where(lane == row, shifted(cells, row + 1), last)
        out_ref[0, start : start + group] = first.astype(BF16)
        out_ref[1, start : start + group] = last.astype(BF16)


def widen_row(load, halo_ref, row, start, group, width):
    lane = lax.broadcasted_iota(jnp.int32, (group, width), 1)
    cells = load(row, start, group)
    wide = cells.astype(F32)
    left = shifted(halo_ref[0, start : start + group].astype(F32), lax.rem(width - row, width))
    right = shifted(halo_ref[1, start : start + group].astype(F32), width - 1 - row)
    before = jnp.where(lane == 0, left, shifted(wide, 1)).astype(BF16)
    after = jnp.where(lane == width - 1, right, shifted(wide, width - 1)).astype(BF16)
    return before, cells, after


def padded_loader(inner, halo, height):
    def load(row, start, group):
        if isinstance(row, int) and row in (0, height + 1):
            return halo[min(row, 1), start : start + group]
        return inner[row - 1, start : start + group]

    return load


def layer_kernel(
    lats, halves, deep, wide_deep, in_ref, we_ref, wf_ref, wr_ref, reb_ref, feat_ref, grad_ref,
    xg, hs, hrow, pre, inhalo, hidhalo, packed, arrived, hpacked, harrived, accx, accg, parts,
    from_pair, lon_out, from_lon, lat_out, from_lat, *sems,
):
    height, both, width = in_ref.shape
    hid = hrow.shape[1]
    lons = 2 * halves
    band = 3 * wide_deep
    lat = lax.axis_index("lat")
    lon = lax.axis_index("lon")
    half = lax.div(lon, 2)
    core = lax.rem(lon, 2)
    other = 1 - core
    below_top = lax.div(lat + lats - 1, lats)
    above_end = lax.div(2 * lats - 2 - lat, lats)

    def lon_peer(step):
        return (lat, lax.rem(half + step, halves) * 2 + core)

    def lat_peer(step):
        return (lax.rem(lat + step, lats), lon)

    pair = (lat, half * 2 + other)
    outer = (lat, lax.rem(lon + lons + 2 * core - 1, lons))
    west = (lat, lax.rem(lon + lons - 1, lons))
    east = (lat, lax.rem(lon + 1, lons))
    north = (lat - below_top, lax.rem(lon + (1 - below_top) * halves, lons))
    south = (lat + above_end, lax.rem(lon + (1 - above_end) * halves, lons))

    barrier = pltpu.get_barrier_semaphore()
    peers = [pair, outer]
    peers += [lon_peer(step) for step in range(1, halves)]
    peers += [lat_peer(step) for step in range(1, lats)]
    for peer in peers:
        pl.semaphore_signal(barrier, inc=1, device_id=peer, device_id_type=MESH)

    def send(src, dst, phase, send_slot, recv_slot, peer):
        copy = pltpu.make_async_remote_copy(
            src_ref=src,
            dst_ref=dst,
            send_sem=sems[2 * phase].at[send_slot],
            recv_sem=sems[2 * phase + 1].at[recv_slot],
            device_id=peer,
            device_id_type=MESH,
        )
        copy.start()
        return copy

    def swap_columns(source, target, phase):
        return [
            send(source.at[1], target.at[0], phase, 0, 0, east),
            send(source.at[0], target.at[1], phase, 1, 1, west),
        ]

    def swap_rows(rows, halo, phase):
        return [
            send(rows.at[0], halo.at[below_top], phase, 0, below_top, north),
            send(rows.at[height - 1], halo.at[1 - above_end], phase, 1, 1 - above_end, south),
        ]

    def wait_rows(copies, halo, phase):
        for copy in copies:
            copy.wait_send()
        for slot in range(2):
            edge = halo.at[slot]
            pltpu.make_async_copy(edge, edge, sems[2 * phase + 1].at[slot]).wait()

    load_in = padded_loader(in_ref, inhalo, height)
    load_hid = padded_loader(hrow, hidhalo, height)
    pl.semaphore_wait(barrier, len(peers))
    copies = swap_rows(in_ref, inhalo, 13)
    accx[...] = jnp.zeros_like(accx)
    accg[...] = jnp.zeros_like(accg)
    wait_rows(copies, inhalo, 13)
    pack_columns(load_in, packed, both, both // 2, height + 2, width)
    copies = swap_columns(packed, arrived, 12)
    for copy in copies:
        copy.wait()

    def widen_in(row):
        before, cells, after = widen_row(load_in, arrived, row, 0, wide_deep, width)
        for place, value in enumerate((before, cells, after)):
            xg[row, place * wide_deep : (place + 1) * wide_deep] = value
        before, cells, after = widen_row(load_in, arrived, row, wide_deep, wide_deep, width)
        for place, value in enumerate((after, cells, before)):
            xg[row, band + place * wide_deep : band + (place + 1) * wide_deep] = value

    widen_in(0)
    widen_in(height + 1)

    @pl.loop(1, height + 1)
    def _(row):
        widen_in(row)

    def window(ref, row, start, count):
        return jnp.concatenate(
            [
                ref[pl.ds(row + place, 3), start : start + count].reshape(3 * count, width)
                for place in range(rows)
            ],
            axis=1,
        )

    def first_step(step):
        row = step * rows
        in_cols = window(xg, row, 0, band)
        cot_cols = window(xg, row, band, band)
        pre_act = dot(we_ref[...], in_cols, ((1,), (0,)))
        pre[step] = pre_act
        hidden = (pre_act * (1.0 / (1.0 + jnp.exp(-pre_act)))).astype(BF16)
        for place in range(rows):
            hrow[row + place] = hidden[:, place * width : (place + 1) * width]
        accg[...] += dot(cot_cols, hidden, ((1,), (1,)))

    def second_step(step, extra):
        row = step * rows
        in_cols = window(xg, row, 0, band)
        cot_cols = window(xg, row, band, band)
        pre_act = pre[step]
        logistic = 1.0 / (1.0 + jnp.exp(-pre_act))
        feat = dot(wf_ref[...], cot_cols, ((1,), (0,)))
        if extra is not None:
            feat = feat + extra
        feat = feat.astype(BF16)
        for place in range(rows):
            feat_ref[row + place] = feat[:, place * width : (place + 1) * width]
        pre_grad = (
            feat.astype(F32) * logistic * (1.0 + pre_act * (1.0 - logistic))
        ).astype(BF16)
        accx[...] += dot(in_cols, pre_grad, ((1,), (1,)))

    rows = 4
    steps = height // rows
    ends = ((0, below_top, 2 * band, 0), (1, above_end, 0, height - 1))
    at_poles = []
    for slot, inside, start, row in ends:
        edge = xg[slot * (height + 1), band:]
        at_poles.append(jnp.where(inside == 0, edge, jnp.zeros_like(edge)))
        xg[slot * (height + 1), band:] = jnp.where(inside == 0, jnp.zeros_like(edge), edge)
    first_step(0)
    first_step(steps - 1)
    row_copies = swap_rows(hrow, hidhalo, 15)

    @pl.loop(1, steps - 1)
    def _(step):
        first_step(step)

    for slot, inside, start, row in ends:
        accg[start : start + band] += dot(at_poles[slot], hrow[row], ((1,), (1,)))

    lane = hid // 2
    lane_rows = parts.shape[2]
    lon_rows = lane_rows // halves
    lat_rows = lon_rows // lats

    def fill(stream, acc, backward):
        for tap in range(9):
            row_tap, col_tap = divmod(tap, 3)
            source = ((2 - row_tap) * 3 + col_tap if backward else tap) * wide_deep
            for side in range(2):
                parts[stream, side, tap * deep : (tap + 1) * deep] = acc[
                    source : source + deep, side * lane : (side + 1) * lane
                ]
        used = 9 * deep
        if lane_rows > used:
            for side in range(2):
                parts[stream, side, used:] = jnp.zeros((lane_rows - used, lane), F32)

    def piece(index, count):
        return pl.ds(pl.multiple_of(index * count, 16), count)

    order = sorted(range(1, lats), key=lambda step: abs(2 * step - lats))

    def start_pair(stream):
        copies = {}
        for step in list(range(1, halves)) + [0]:
            part = piece(lax.rem(half + step, halves), lon_rows)
            copies[step] = send(
                parts.at[stream, other, part], from_pair.at[stream, part], stream * 6, step, step, pair
            )
        return copies

    def start_lon(stream, copies):
        onward = {}
        for step in range(1, halves):
            copies[step].wait()
            target = lax.rem(half + step, halves)
            part = piece(target, lon_rows)
            lon_out[stream, part] = (parts[stream, core, part] + from_pair[stream, part]).astype(LINK)
            for turn in order + [0]:
                there = lax.rem(lat + turn, lats)
                onward[step, turn] = send(
                    lon_out.at[stream, piece(target * lats + there, lat_rows)],
                    from_lon.at[stream, step - 1, piece(there, lat_rows)],
                    stream * 6 + 1, (step - 1) * lats + turn, (step - 1) * lats + turn, lon_peer(step),
                )
        copies[0].wait()
        return onward

    def lon_total(stream, copies, turn):
        there = lax.rem(lat + turn, lats)
        part = piece(half * lats + there, lat_rows)
        total = parts[stream, core, part] + from_pair[stream, part]
        for step in range(1, halves):
            copies[step, turn].wait()
            total = total + from_lon[stream, step - 1, piece(there, lat_rows)].astype(F32)
        return total

    def start_lat(stream, copies):
        onward = []
        for turn in order:
            there = piece(lax.rem(lat + turn, lats), lat_rows)
            lat_out[stream, there] = lon_total(stream, copies, turn).astype(LINK)
            onward.append(
                send(
                    lat_out.at[stream, there], from_lat.at[stream, turn - 1],
                    stream * 6 + 2, turn - 1, turn - 1, lat_peer(turn),
                )
            )
        return onward, lon_total(stream, copies, 0)

    def spread(stream, turn, lon_copies, pair_copies):
        there = lax.rem(lat + lats - turn, lats)
        mine = grad_ref.at[stream, core, piece(half * lats + there, lat_rows)]
        for step in range(1, halves):
            slot = (step - 1) * lats + turn
            lon_copies[step, turn] = send(mine, mine, stream * 6 + 4, slot, slot, lon_peer(step))
        pair_copies.append(send(mine, mine, stream * 6 + 5, turn, turn, pair))

    def start_lat_gather(stream, started):
        copies, total = started
        for turn, copy in zip(order, copies):
            copy.wait()
            total = total + from_lat[stream, turn - 1].astype(F32)
        place = piece(half * lats + lat, lat_rows)
        grad_ref[stream, core, place] = total.astype(grad_ref.dtype)
        mine = grad_ref.at[stream, core, place]
        copies = [
            send(mine, mine, stream * 6 + 3, turn - 1, turn - 1, lat_peer(turn)) for turn in order
        ]
        lon_copies, pair_copies = {}, []
        spread(stream, 0, lon_copies, pair_copies)
        return copies, lon_copies, pair_copies

    def start_spread(stream, started):
        copies, lon_copies, pair_copies = started
        for turn, copy in reversed(list(zip(order, copies))):
            copy.wait()
            spread(stream, turn, lon_copies, pair_copies)
        return lon_copies, pair_copies

    def start_pair_gather(stream, started):
        lon_copies, pair_copies = started
        for turn in [0] + order[::-1]:
            for step in range(1, halves):
                lon_copies[step, turn].wait()
                source = lax.rem(half + halves - step, halves)
                there = lax.rem(lat + lats - turn, lats)
                mine = grad_ref.at[stream, core, piece(source * lats + there, lat_rows)]
                slot = step * lats + turn
                pair_copies.append(send(mine, mine, stream * 6 + 5, slot, slot, pair))
        return pair_copies

    fill(0, accg, True)
    gen_copies = start_pair(0)
    wait_rows(row_copies, hidhalo, 15)
    pack_columns(load_hid, hpacked, hid, 64, height + 2, width)
    column_copies = swap_columns(hpacked, harrived, 14)
    gen_copies = start_lon(0, gen_copies)

    @pl.loop(1, steps - 1)
    def _(step):
        second_step(step, None)

    gen_copies = start_lat(0, gen_copies)
    open_gap = jnp.zeros((hid, (rows - 1) * width), F32)
    for slot, inside, start, row in ends:
        term = dot(wf_ref[:, start : start + band], at_poles[slot], ((1,), (0,)))
        both_terms = [term, open_gap] if slot == 0 else [open_gap, term]
        second_step(row // rows, jnp.concatenate(both_terms, axis=1))
    fill(1, accx, False)
    enc_copies = start_pair(1)
    for copy in column_copies:
        copy.wait()
    gen_copies = start_lat_gather(0, gen_copies)
    enc_copies = start_lon(1, enc_copies)

    def widen_hid(row):
        for start in range(0, hid, 64):
            parts_row = widen_row(load_hid, harrived, row, start, 64, width)
            for place, value in enumerate(parts_row):
                hs[row, place * hid + start : place * hid + start + 64] = value

    widen_hid(0)
    widen_hid(height + 1)

    @pl.loop(1, height // 2)
    def _(row):
        widen_hid(row)

    enc_copies = start_lat(1, enc_copies)

    @pl.loop(height // 2, height + 1)
    def _(row):
        widen_hid(row)

    gen_copies = start_spread(0, gen_copies)
    enc_copies = start_lat_gather(1, enc_copies)

    @pl.loop(0, steps)
    def _(step):
        value = dot(wr_ref[...], window(hs, step * rows, 0, 3 * hid), ((1,), (0,))).astype(BF16)
        for place in range(rows):
            reb_ref[step * rows + place] = value[:, place * width : (place + 1) * width]

    gen_copies = start_pair_gather(0, gen_copies)
    enc_copies = start_spread(1, enc_copies)
    enc_copies = start_pair_gather(1, enc_copies)
    for copy in gen_copies + enc_copies:
        copy.wait()


def on_device(fields, enc_kernel, gen_kernel, recon_grad):
    in_count, height, width = fields.shape
    hid = enc_kernel.shape[2]
    deep = -(-in_count // 8) * 8
    wide_deep = -(-in_count // 16) * 16
    extra = wide_deep - in_count
    lats = lax.axis_size("lat")
    lons = lax.axis_size("lon")
    halves = lons // 2
    room = ((0, 0), (0, extra), (0, 0))
    stacked = jnp.concatenate(
        [
            jnp.pad(fields.transpose(1, 0, 2), room),
            jnp.pad(recon_grad.transpose(1, 0, 2), room),
        ],
        axis=1,
    )
    band = 3 * wide_deep
    enc_flat = jnp.pad(enc_kernel, ((0, 0), (0, 0), (0, 0), (0, extra)))
    enc_flat = enc_flat.transpose(2, 0, 1, 3).reshape(hid, 3 * band)
    gen_taps = jnp.pad(gen_kernel, ((0, 0), (0, 0), (0, extra), (0, 0)))
    back_flat = gen_taps[::-1].transpose(3, 0, 1, 2).reshape(hid, 3 * band)
    gen_flat = gen_taps.transpose(2, 0, 1, 3).reshape(wide_deep, 9 * hid)
    lane = hid // 2
    lat_rows = -(-9 * deep // (halves * lats * 16)) * 16
    lon_rows = lats * lat_rows
    lane_rows = halves * lon_rows
    hops = (halves - 1) * lats
    counts = [halves, hops, lats - 1, lats - 1, hops, halves * lats] * 2 + [2] * 4
    rebuilt, feat, summed = pl.pallas_call(
        functools.partial(layer_kernel, lats, halves, deep, wide_deep),
        out_shape=[
            jax.ShapeDtypeStruct((height, wide_deep, width), BF16),
            jax.ShapeDtypeStruct((height, hid, width), BF16),
            jax.ShapeDtypeStruct((2, 2, lane_rows, lane), BF16),
        ],
        in_specs=[pl.BlockSpec(memory_space=pltpu.VMEM)] * 4,
        out_specs=[pl.BlockSpec(memory_space=pltpu.VMEM)] * 3,
        scratch_shapes=[
            pltpu.VMEM((height + 2, 2 * band, width), BF16),
            pltpu.VMEM((height + 2, 3 * hid, width), BF16),
            pltpu.VMEM((height, hid, width), BF16),
            pltpu.VMEM((height // 4, hid, 4 * width), F32),
            pltpu.VMEM((2, 2 * wide_deep, width), BF16),
            pltpu.VMEM((2, hid, width), BF16),
            pltpu.VMEM((2, 2 * wide_deep, width), BF16),
            pltpu.VMEM((2, 2 * wide_deep, width), BF16),
            pltpu.VMEM((2, hid, width), BF16),
            pltpu.VMEM((2, hid, width), BF16),
            pltpu.VMEM((3 * band, hid), F32),
            pltpu.VMEM((3 * band, hid), F32),
            pltpu.VMEM((2, 2, lane_rows, lane), F32),
            pltpu.VMEM((2, lane_rows, lane), F32),
            pltpu.VMEM((2, lane_rows, lane), LINK),
            pltpu.VMEM((2, halves - 1, lon_rows, lane), LINK),
            pltpu.VMEM((2, lon_rows, lane), LINK),
            pltpu.VMEM((2, lats - 1, lat_rows, lane), LINK),
        ]
        + [pltpu.SemaphoreType.DMA((count,)) for count in counts for _ in range(2)],
        compiler_params=pltpu.CompilerParams(
            collective_id=0, has_side_effects=True, vmem_limit_bytes=48 << 20
        ),
    )(stacked, enc_flat, back_flat, gen_flat)
    norm_scale = 1.0 / jnp.sqrt(F32(height * lats * width * lons))
    grads = jnp.concatenate([summed[:, 0, : 9 * deep], summed[:, 1, : 9 * deep]], axis=2)
    grads = grads.reshape(2, 3, 3, deep, hid)[:, :, :, :in_count].astype(F32) * norm_scale
    return (
        rebuilt[:, :in_count].transpose(1, 0, 2),
        feat.transpose(1, 0, 2),
        grads[1].transpose(0, 1, 3, 2),
        grads[0],
    )


def solution(mesh):
    return jax.shard_map(
        on_device,
        mesh=mesh,
        in_specs=(P(None, "lat", "lon"), P(), P(), P(None, "lat", "lon")),
        out_specs=(P(None, "lat", "lon"), P(None, "lat", "lon"), P(), P()),
        check_vma=False,
    )
```

time: 62.3 us -> 55 us (0.88)
  Pallas kernels: 54.5 us -> 47.2 us
    pallas_call x1, Pallas kernels: 54.5 us -> 47.2 us  [on_device(): pl.pallas_call(functools.partial(layer_kernel, lats, halves, deep, wide_d...]
where the time goes in v3:
time: 55 us; the launch traced here: 54.9 us
  Pallas kernels  47.2 us (86%)
  local copies, waits for them, and re-layouts  6.7 us (12%)
  between operations  0.75 us (1%)
    pallas_call x1, Pallas kernels, on_device(): pl.pallas_call(functools.partial(layer_kernel, lats, halves, deep, wide_d...  47.2 us
    unnamed x8, local copies, waits for them, and re-layouts  3.15 us
    squeeze x1, local copies, waits for them, and re-layouts, on_device(): grads[0]  1.17 us

profile of v3, /device:TPU:0, one launch (start us, length us, event | category | flops | bytes accessed | tf_op | source)
XLA Modules:
  0.0 54.9 jit_solution(4354679559834599455)
XLA Ops:
  0.6 0.0 copy-start.1
  0.6 0.0 copy-start.2
  0.7 1.1 %pad.17 = bf16[3,3,256,80]{2,3,1,0:T(8,128)(2,1)S(1)} pad(bf16[3,3,256,69]{2,3,1,0:T(8,128)(2,1)} %param.5, bf16[]{:T(256)} %constant.1.clone.1), padding=0_0x0_0x0_0x0_11 | pad | bytes 686594 | tf_op jit(solution)/shard_map/jit(_pad)/pad | solution.py:398
  1.7 0.2 copy.18.we_ref
  1.9 0.0 copy-done.1
  1.9 0.0 copy-done.2
  1.9 0.0 copy-start
  1.9 0.2 copy_bitcast_fusion
  2.1 0.1 fusion.2.in_ref
  2.1 0.7 %copy-done = bf16[3,3,69,256]{3,2,1,0:T(8,128)(2,1)S(1)} copy-done((bf16[3,3,69,256]{3,2,1,0:T(8,128)(2,1)S(1)}, bf16[3,3,69,256]{3,2,1,0:T(8,128)(2,1)}, u32[]{:S(2)}) %copy-start) | copy-done | bytes 317976
  2.9 0.3 copy.17
  3.2 0.4 reshape.24.wr_ref
  3.7 0.2 copy.19.wf_ref
  3.8 47.2 %shard_map.75 = (bf16[16,80,128]{2,1,0:T(8,128)(2,1)S(1)}, bf16[16,256,128]{2,1,0:T(8,128)(2,1)S(1)}, bf16[2,2,768,128]{3,2,1,0:T(8,128)(2,1)S(1)}) custom-call(bf16[16,160,128]{2,1,0:T(8,128)(2,1)S(1)} %fusion.2.in_ref, bf16[256,720]{1,0:T(8,128)(2,1)S(1)} %copy.18.we_ref, bf16[256,720]{1,0:T(8,128)(2,1)S(1)} %copy.19.wf_ref, ...), custom_call_target="tpu_custom_call" | custom-call | tf_op jit(solution)/shard_map/pallas_call | solution.py:409
  51.1 0.7 %copy.20 = bf16[69,16,128]{2,1,0:T(8,128)(2,1)} copy(bf16[69,16,128]{2,0,1:T(8,128)(2,1)S(1)} %slice_bitcast_fusion.2) | data formatting | bytes 565248
  51.9 1.6 %copy.21 = bf16[256,16,128]{2,1,0:T(8,128)(2,1)} copy(bf16[256,16,128]{2,0,1:T(8,128)(2,1)S(1)} %bitcast.23) | data formatting | bytes 2097152
  53.6 0.1 convert_multiply_fusion
  53.7 1.2 %slice_bitcast_fusion = (f32[3,3,69,256]{3,2,1,0:T(8,128)}, f32[3,3,256,69]{2,3,1,0:T(8,128)}) fusion(f32[2,3,3,69,256]{4,3,2,1,0:T(8,128)S(1)} %convert_multiply_fusion), kind=kLoop, calls=%fused_computation.5 | loop fusion | bytes 2543616 | tf_op jit(solution)/shard_map/squeeze | solution.py:450
  (4 shorter events, 0.1 us)
Async XLA Ops:
  0.6 1.3 %copy-start.1 = (bf16[69,16,128]{2,1,0:T(8,128)(2,1)S(1)}, bf16[69,16,128]{2,1,0:T(8,128)(2,1)}, u32[]{:S(2)}) copy-start(bf16[69,16,128]{2,1,0:T(8,128)(2,1)} %param.7) | copy-start | bytes 847876
  0.6 1.3 %copy-start.2 = (bf16[69,16,128]{2,1,0:T(8,128)(2,1)S(1)}, bf16[69,16,128]{2,1,0:T(8,128)(2,1)}, u32[]{:S(2)}) copy-start(bf16[69,16,128]{2,1,0:T(8,128)(2,1)} %param.4) | copy-start | bytes 847876
  1.9 1.0 %copy-start = (bf16[3,3,69,256]{3,2,1,0:T(8,128)(2,1)S(1)}, bf16[3,3,69,256]{3,2,1,0:T(8,128)(2,1)}, u32[]{:S(2)}) copy-start(bf16[3,3,69,256]{3,2,1,0:T(8,128)(2,1)} %param.6) | copy-start | bytes 953860

commit v4 on v3

--- a/solution.py
+++ b/solution.py
@@ -56,7 +56,7 @@
 
 def layer_kernel(
     lats, halves, deep, wide_deep, in_ref, we_ref, wf_ref, wr_ref, reb_ref, feat_ref, grad_ref,
-    xg, hs, hrow, pre, inhalo, hidhalo, packed, arrived, hpacked, harrived, accx, accg, parts,
+    xg, hs, hrow, pre, hidhalo, packed, arrived, hpacked, harrived, accx, accg, parts,
     from_pair, lon_out, from_lon, lat_out, from_lat, *sems,
 ):
     height, both, width = in_ref.shape
@@ -122,30 +122,34 @@
             edge = halo.at[slot]
             pltpu.make_async_copy(edge, edge, sems[2 * phase + 1].at[slot]).wait()
 
-    load_in = padded_loader(in_ref, inhalo, height)
+    def load_in(row, start, group):
+        return in_ref[row, start : start + group]
+
     load_hid = padded_loader(hrow, hidhalo, height)
+    pack_columns(load_in, packed, both, both // 2, height, width)
     pl.semaphore_wait(barrier, len(peers))
-    copies = swap_rows(in_ref, inhalo, 13)
+    copies = swap_columns(packed, arrived, 12)
     accx[...] = jnp.zeros_like(accx)
     accg[...] = jnp.zeros_like(accg)
-    wait_rows(copies, inhalo, 13)
-    pack_columns(load_in, packed, both, both // 2, height + 2, width)
-    copies = swap_columns(packed, arrived, 12)
     for copy in copies:
         copy.wait()
 
     def widen_in(row):
         before, cells, after = widen_row(load_in, arrived, row, 0, wide_deep, width)
         for place, value in enumerate((before, cells, after)):
-            xg[row, place * wide_deep : (place + 1) * wide_deep] = value
+            xg[row + 1, place * wide_deep : (place + 1) * wide_deep] = value
         before, cells, after = widen_row(load_in, arrived, row, wide_deep, wide_deep, width)
         for place, value in enumerate((after, cells, before)):
-            xg[row, band + place * wide_deep : band + (place + 1) * wide_deep] = value
+            xg[row + 1, band + place * wide_deep : band + (place + 1) * wide_deep] = value
 
     widen_in(0)
-    widen_in(height + 1)
-
-    @pl.loop(1, height + 1)
+    widen_in(height - 1)
+    copies = [
+        send(xg.at[1], xg.at[below_top * (height + 1)], 13, 0, below_top, north),
+        send(xg.at[height], xg.at[(1 - above_end) * (height + 1)], 13, 1, 1 - above_end, south),
+    ]
+
+    @pl.loop(1, height - 1)
     def _(row):
         widen_in(row)
 
@@ -189,6 +193,16 @@
     rows = 4
     steps = height // rows
     ends = ((0, below_top, 2 * band, 0), (1, above_end, 0, height - 1))
+
+    @pl.loop(1, steps - 1)
+    def _(step):
+        first_step(step)
+
+    for copy in copies:
+        copy.wait_send()
+    for slot in range(2):
+        edge = xg.at[slot * (height + 1)]
+        pltpu.make_async_copy(edge, edge, sems[27].at[slot]).wait()
     at_poles = []
     for slot, inside, start, row in ends:
         edge = xg[slot * (height + 1), band:]
@@ -197,11 +211,6 @@
     first_step(0)
     first_step(steps - 1)
     row_copies = swap_rows(hrow, hidhalo, 15)
-
-    @pl.loop(1, steps - 1)
-    def _(step):
-        first_step(step)
-
     for slot, inside, start, row in ends:
         accg[start : start + band] += dot(at_poles[slot], hrow[row], ((1,), (1,)))
 
@@ -320,16 +329,12 @@
 
     fill(0, accg, True)
     gen_copies = start_pair(0)
-    wait_rows(row_copies, hidhalo, 15)
-    pack_columns(load_hid, hpacked, hid, 64, height + 2, width)
-    column_copies = swap_columns(hpacked, harrived, 14)
-    gen_copies = start_lon(0, gen_copies)
 
     @pl.loop(1, steps - 1)
     def _(step):
         second_step(step, None)
 
-    gen_copies = start_lat(0, gen_copies)
+    gen_copies = start_lon(0, gen_copies)
     open_gap = jnp.zeros((hid, (rows - 1) * width), F32)
     for slot, inside, start, row in ends:
         term = dot(wf_ref[:, start : start + band], at_poles[slot], ((1,), (0,)))
@@ -337,10 +342,15 @@
         second_step(row // rows, jnp.concatenate(both_terms, axis=1))
     fill(1, accx, False)
     enc_copies = start_pair(1)
+    gen_copies = start_lat(0, gen_copies)
+    enc_copies = start_lon(1, enc_copies)
+    wait_rows(row_copies, hidhalo, 15)
+    pack_columns(load_hid, hpacked, hid, 64, height + 2, width)
+    column_copies = swap_columns(hpacked, harrived, 14)
+    enc_copies = start_lat(1, enc_copies)
+    gen_copies = start_lat_gather(0, gen_copies)
     for copy in column_copies:
         copy.wait()
-    gen_copies = start_lat_gather(0, gen_copies)
-    enc_copies = start_lon(1, enc_copies)
 
     def widen_hid(row):
         for start in range(0, hid, 64):
@@ -351,18 +361,12 @@
     widen_hid(0)
     widen_hid(height + 1)
 
-    @pl.loop(1, height // 2)
+    @pl.loop(1, height + 1)
     def _(row):
         widen_hid(row)
 
-    enc_copies = start_lat(1, enc_copies)
-
-    @pl.loop(height // 2, height + 1)
-    def _(row):
-        widen_hid(row)
-
+    enc_copies = start_lat_gather(1, enc_copies)
     gen_copies = start_spread(0, gen_copies)
-    enc_copies = start_lat_gather(1, enc_copies)
 
     @pl.loop(0, steps)
     def _(step):
@@ -420,7 +424,6 @@
             pltpu.VMEM((height + 2, 3 * hid, width), BF16),
             pltpu.VMEM((height, hid, width), BF16),
             pltpu.VMEM((height // 4, hid, 4 * width), F32),
-            pltpu.VMEM((2, 2 * wide_deep, width), BF16),
             pltpu.VMEM((2, hid, width), BF16),
             pltpu.VMEM((2, 2 * wide_deep, width), BF16),
             pltpu.VMEM((2, 2 * wide_deep, width), BF16),

time: 55 us -> 49.5 us (0.900)
  Pallas kernels: 47.2 us -> 41.7 us
    pallas_call x1, Pallas kernels: 47.2 us -> 41.7 us  [on_device(): pl.pallas_call(functools.partial(layer_kernel, lats, halves, deep, wide_d...]
where the time goes in v4:
time: 49.5 us; the launch traced here: 49.3 us
  Pallas kernels  41.7 us (84%)
  local copies, waits for them, and re-layouts  6.7 us (14%)
  between operations  0.75 us (2%)
    pallas_call x1, Pallas kernels, on_device(): pl.pallas_call(functools.partial(layer_kernel, lats, halves, deep, wide_d...  41.7 us
    unnamed x8, local copies, waits for them, and re-layouts  3.15 us
    squeeze x1, local copies, waits for them, and re-layouts, on_device(): grads[0]  1.17 us
    pad x1, local copies, waits for them, and re-layouts, on_device(): enc_flat = jnp.pad(enc_kernel, ((0, 0), (0, 0), (0, 0), (0, extra)))  1.06 us

profile of v4, /device:TPU:0, one launch (start us, length us, event | category | flops | bytes accessed | tf_op | source)
XLA Modules:
  0.0 49.3 jit_solution(5989024301998651907)
XLA Ops:
  0.6 0.0 copy-start.1
  0.6 0.0 copy-start.2
  0.7 1.1 %pad.17 = bf16[3,3,256,80]{2,3,1,0:T(8,128)(2,1)S(1)} pad(bf16[3,3,256,69]{2,3,1,0:T(8,128)(2,1)} %param.5, bf16[]{:T(256)} %constant.1.clone.1), padding=0_0x0_0x0_0x0_11 | pad | bytes 686594 | tf_op jit(solution)/shard_map/jit(_pad)/pad | solution.py:402
  1.7 0.2 copy.18.we_ref
  1.9 0.0 copy-done.1
  1.9 0.0 copy-done.2
  1.9 0.0 copy-start
  1.9 0.2 copy_bitcast_fusion
  2.1 0.1 fusion.2.in_ref
  2.1 0.7 %copy-done = bf16[3,3,69,256]{3,2,1,0:T(8,128)(2,1)S(1)} copy-done((bf16[3,3,69,256]{3,2,1,0:T(8,128)(2,1)S(1)}, bf16[3,3,69,256]{3,2,1,0:T(8,128)(2,1)}, u32[]{:S(2)}) %copy-start) | copy-done | bytes 317976
  2.9 0.3 copy.17
  3.2 0.4 reshape.24.wr_ref
  3.7 0.2 copy.19.wf_ref
  3.8 41.7 %shard_map.75 = (bf16[16,80,128]{2,1,0:T(8,128)(2,1)S(1)}, bf16[16,256,128]{2,1,0:T(8,128)(2,1)S(1)}, bf16[2,2,768,128]{3,2,1,0:T(8,128)(2,1)S(1)}) custom-call(bf16[16,160,128]{2,1,0:T(8,128)(2,1)S(1)} %fusion.2.in_ref, bf16[256,720]{1,0:T(8,128)(2,1)S(1)} %copy.18.we_ref, bf16[256,720]{1,0:T(8,128)(2,1)S(1)} %copy.19.wf_ref, ...), custom_call_target="tpu_custom_call" | custom-call | tf_op jit(solution)/shard_map/pallas_call | solution.py:413
  45.6 0.7 %copy.20 = bf16[69,16,128]{2,1,0:T(8,128)(2,1)} copy(bf16[69,16,128]{2,0,1:T(8,128)(2,1)S(1)} %slice_bitcast_fusion.2) | data formatting | bytes 565248
  46.3 1.6 %copy.21 = bf16[256,16,128]{2,1,0:T(8,128)(2,1)} copy(bf16[256,16,128]{2,0,1:T(8,128)(2,1)S(1)} %bitcast.23) | data formatting | bytes 2097152
  48.0 0.1 convert_multiply_fusion
  48.2 1.2 %slice_bitcast_fusion = (f32[3,3,69,256]{3,2,1,0:T(8,128)}, f32[3,3,256,69]{2,3,1,0:T(8,128)}) fusion(f32[2,3,3,69,256]{4,3,2,1,0:T(8,128)S(1)} %convert_multiply_fusion), kind=kLoop, calls=%fused_computation.5 | loop fusion | bytes 2543616 | tf_op jit(solution)/shard_map/squeeze | solution.py:453
  (4 shorter events, 0.1 us)
Async XLA Ops:
  0.6 1.3 %copy-start.1 = (bf16[69,16,128]{2,1,0:T(8,128)(2,1)S(1)}, bf16[69,16,128]{2,1,0:T(8,128)(2,1)}, u32[]{:S(2)}) copy-start(bf16[69,16,128]{2,1,0:T(8,128)(2,1)} %param.7) | copy-start | bytes 847876
  0.6 1.3 %copy-start.2 = (bf16[69,16,128]{2,1,0:T(8,128)(2,1)S(1)}, bf16[69,16,128]{2,1,0:T(8,128)(2,1)}, u32[]{:S(2)}) copy-start(bf16[69,16,128]{2,1,0:T(8,128)(2,1)} %param.4) | copy-start | bytes 847876
  1.9 1.0 %copy-start = (bf16[3,3,69,256]{3,2,1,0:T(8,128)(2,1)S(1)}, bf16[3,3,69,256]{3,2,1,0:T(8,128)(2,1)}, u32[]{:S(2)}) copy-start(bf16[3,3,69,256]{3,2,1,0:T(8,128)(2,1)} %param.6) | copy-start | bytes 953860
